TPU v7x, 768 devices: a whole 4x8x12 slice. The times are simulated.
768 devices in a mesh: member: 8 (over y), domain: 12 (over z), role: 8 (over x, core).
Axes of the slice: x: 4, y: 8, z: 12, core: 2. Of those that a mesh axis runs over, the one named last changes fastest.
Arguments:
- ensemble: float32 [256, 768, 1024], P('member', 'domain', 'role'), may hold values from -6 to 6
- diffusion: float32 [768, 1024], P('domain', 'role'), may hold values from 0.02 to 0.1
- drift_rows: float32 [768, 1024], P('domain', 'role'), may hold values from 0.05 to 0.3
- drift_cols: float32 [768, 1024], P('domain', 'role'), may hold values from 0.05 to 0.3
- observed_cells: int32 [12, 1024], P('domain'), may hold values from 0 to 65535
- observed_count: int32 [12], P('domain'), may hold values from 256 to 1024
- observed_values: float32 [12, 1024], P('domain'), may hold values from -6 to 6
- observed_weights: float32 [12, 1024], P('domain'), may hold values from 0.5 to 4
Outputs:
- analysis: float32 [256, 768, 1024], P('member', 'domain', 'role')
All inputs are finite; a program needn't handle non-finite values.
Results may differ from a plain program's by a relative error of at most 0.0003.
Values sent between devices are 32-bit elements; how exact they have to be, the bound alone decides.
A program may use at most 64 MiB of HBM per device.

v0:
```python
import jax
import jax.numpy as jnp
from jax import lax
from jax.sharding import Mesh
from jax.sharding import PartitionSpec as P

STEPS = 4
ITERS = 6
ROLE = ("role_0", "role_1")
MEMBER_ROLE = ("member", "role_0", "role_1")


precise = lax.Precision.HIGHEST


def with_halo(value, sides, width):
    edges = {}
    for axis, dim in sides:
        size, length = (lax.axis_size(axis), value.shape[dim])
        up = [(i, (i + 1) % size) for i in range(size)]
        last = lax.slice_in_dim(value, length - width, length, axis=dim)
        initial = lax.slice_in_dim(value, 0, width, axis=dim)
        edges[dim] = (
            lax.ppermute(last, axis, up),
            lax.ppermute(initial, axis, [(b, a) for a, b in up]),
        )
    done = []
    for _, dim in sides:
        low, high = edges[dim]
        around = [(width, width) if d in done else (0, 0) for d in range(value.ndim)]
        value = jnp.concatenate([jnp.pad(low, around), value, jnp.pad(high, around)], axis=dim)
        done.append(dim)
    return value


def split_up(value, dim, size):
    before, after = (value.shape[:dim], value.shape[dim + 1 :])
    return jnp.moveaxis(value.reshape(*before, size, -1, *after), dim, 0)


def laid_out(parts, dim):
    lengths = list(parts.shape[1:])
    lengths[dim] *= parts.shape[0]
    return jnp.moveaxis(parts, 0, dim).reshape(lengths)


def joined_exchange(value, axis, axes, splits, concats):
    sizes = [lax.axis_size(a) for a in axes]
    parts = split_up(value, splits[0], sizes[0])
    parts = jnp.moveaxis(split_up(parts, splits[1] + 1, sizes[1]), 0, 1)
    inside = parts.shape[2:]
    parts = parts.reshape(-1, *inside)
    parts = lax.all_to_all(parts, axis, split_axis=0, concat_axis=0, tiled=True)
    parts = laid_out(parts.reshape(*sizes, *inside), concats[0] + 1)
    return laid_out(parts, concats[1])


def padded_to(lines, size):
    spare = -len(lines) % size
    return jnp.pad(lines, [(0, spare)] + [(0, 0)] * (lines.ndim - 1))


def sum_in_order(parts, axes, order):
    inside = parts.shape[1:]
    parts = parts.reshape(*(lax.axis_size(a) for a in axes), *inside)
    parts = jnp.moveaxis(parts, order, range(len(axes))).reshape(-1, *inside)
    for k in order:
        parts = lax.psum_scatter(parts, axes[k], scatter_dimension=0, tiled=True)
    return parts[0]


def stacked_from(value, axes, order):
    parts = value
    for k in order:
        parts = lax.all_gather(parts, axes[k])
    done = order[::-1]
    back = [done.index(k) for k in range(len(axes))]
    parts = parts.transpose(*back, *range(len(axes), parts.ndim))
    return parts.reshape(-1, *value.shape)


def total_of(value, axes, order):
    size, lines = (lax.axis_size(axes), value.reshape(-1, *value.shape[1:][-1:]))
    parts = padded_to(lines, size).reshape(size, -1, *lines.shape[1:])
    own = sum_in_order(parts, axes, order)
    whole = stacked_from(own, axes, order[::-1]).reshape(-1, *lines.shape[1:])
    return whole[: len(lines)].reshape(value.shape)


def inverse_root(matrix):
    extent = matrix.shape[0]
    identity = jnp.eye(extent, dtype=jnp.float32)
    scaling = jnp.sqrt(jnp.sum(matrix * matrix))
    current = matrix / scaling
    inverse = identity
    for repeat in range(ITERS):
        middle = 0.5 * (3.0 * identity - jnp.dot(inverse, current, precision=precise))
        current = jnp.dot(current, middle, precision=precise)
        inverse = jnp.dot(middle, inverse, precision=precise)
    return (inverse, scaling)


def analysis_weights(gram_sum, innovation):
    extent = gram_sum.shape[0]
    matrix = gram_sum + (extent - 1.0) * jnp.eye(extent, dtype=jnp.float32)
    inverse, scaling = inverse_root(matrix)
    spread = jnp.sqrt((extent - 1.0) / scaling) * inverse
    shifted = (
        jnp.dot(inverse, jnp.dot(inverse, innovation, precision=precise), precision=precise)
        / scaling
    )
    return spread + shifted[:, None]


def shards(
    ensemble,
    diffusion,
    drift_rows,
    drift_cols,
    observed_cells,
    observed_count,
    observed_values,
    observed_weights,
):
    current = ensemble
    for repeat in range(STEPS):
        padded = with_halo(current, (("domain", 1), (ROLE, 2)), 1)
        inner = padded[:, 1:-1, 1:-1]
        ahead_rows = padded[:, 2:, 1:-1]
        behind_rows = padded[:, :-2, 1:-1]
        ahead_cols = padded[:, 1:-1, 2:]
        behind_cols = padded[:, 1:-1, :-2]
        spread = ahead_rows + behind_rows + ahead_cols + behind_cols - 4.0 * inner
        current = (
            inner
            + diffusion * spread
            - drift_rows * (inner - behind_rows)
            - drift_cols * (inner - behind_cols)
        )
    member_groups = lax.axis_size("member")
    role_groups = lax.axis_size(ROLE)
    local_members, rows_local, cols_local = current.shape
    members_all = local_members * member_groups
    own_rows = rows_local // (member_groups * role_groups)
    full_cols = cols_local * role_groups
    position = lax.axis_index("member") * role_groups + lax.axis_index(ROLE)
    cell_index = observed_cells[0]
    counts = observed_count[0]
    values = observed_values[0]
    weights = observed_weights[0]
    row_of = cell_index // full_cols
    col_of = cell_index % full_cols
    owned = row_of // own_rows == position
    usable = owned & (jnp.arange(cell_index.shape[0]) < counts)
    row_local = jnp.where(owned, row_of - position * own_rows, 0)
    received = joined_exchange(current, MEMBER_ROLE, ("member", ROLE), (1, 1), (0, 2))
    observed = received[:, row_local, col_of]
    centre_obs = jnp.mean(observed, axis=0)
    deviation = observed - centre_obs
    weighted = deviation * jnp.where(usable, weights, jnp.float32(0.0))
    gram_sum, innovation = (
        total_of(jnp.dot(weighted, deviation.T, precision=precise), MEMBER_ROLE, (1, 2, 0)),
        total_of(jnp.dot(weighted, values - centre_obs, precision=precise), MEMBER_ROLE, (1, 2, 0)),
    )
    mixing = analysis_weights(gram_sum, innovation)
    centre = jnp.mean(received, axis=0)
    deviation_field = (received - centre).reshape(members_all, -1)
    updated = (
        jnp.einsum("kc,kj->jc", deviation_field, mixing, precision=precise).reshape(received.shape)
        + centre
    )
    returned = joined_exchange(updated, MEMBER_ROLE, ("member", ROLE), (0, 2), (1, 1))
    returned = returned.reshape(local_members, role_groups, member_groups, own_rows, cols_local)
    returned = jnp.transpose(returned, (0, 2, 1, 3, 4)).reshape(
        local_members, rows_local, cols_local
    )
    return returned


def solution(mesh):
    torus = Mesh(
        mesh.devices.reshape(mesh.shape["member"], mesh.shape["domain"], 4, 2),
        ("member", "domain", "role_0", "role_1"),
    )
    return jax.shard_map(
        shards,
        mesh=torus,
        in_specs=(
            P("member", "domain", ROLE),
            P("domain", ROLE),
            P("domain", ROLE),
            P("domain", ROLE),
            P("domain", None),
            P("domain"),
            P("domain", None),
            P("domain", None),
        ),
        out_specs=P("member", "domain", ROLE),
        check_vma=False,
    )
```

profile of v0, /device:TPU:1, one launch (start us, length us, event | category | flops | bytes accessed | tf_op | source)
XLA Modules:
  0.0 360.8 jit_solution(9537483215535917667)
XLA Ops:
  6.5 1.0 fusion.87
  7.5 15.1 %collective-permute-start = (f32[32,1,128]{2,1,0:T(1,128)S(1)}, f32[32,1,128]{2,1,0:T(1,128)S(1)}, u32[]{:S(2)}, u32[]{:S(2)}) collective-permute-start(f32[32,1,128]{2,1,0:T(1,128)S(1)} %get-tuple-element.22), channel_id=1, source_target_pairs={{8,0},{16,8},{24,16},{32,24},{40,32},{48,40},{56,48},{64,56},{72,6... | collective-permute-start | bytes 49160 | tf_op jit(solution)/shard_map/ppermute | solution.py:25
  22.7 1.9 collective-permute-start.1
  24.6 2.1 fusion.86
  27.0 1.0 collective-permute-start.2
  28.4 1.1 collective-permute-start.3
  29.5 1.0 collective-permute-done.2
  31.0 1.4 copy.62
  32.4 2.3 fusion.55
  34.8 4.8 %collective-permute-start.4 = (f32[32,1,128]{2,1,0:T(1,128)S(1)}, f32[32,1,128]{2,1,0:T(1,128)S(1)}, u32[]{:S(2)}, u32[]{:S(2)}) collective-permute-start(f32[32,1,128]{2,1,0:T(1,128)S(1)} %get-tuple-element.18), channel_id=1, source_target_pairs={{8,0},{16,8},{24,16},{32,24},{40,32},{48,40},{56,48},{64,56},{72,6... | collective-permute-start | bytes 49160 | tf_op jit(solution)/shard_map/ppermute | solution.py:25
  39.6 1.9 collective-permute-start.5
  42.3 3.7 %collective-permute-start.6 = (f32[32,64,1]{1,0,2:T(8,128)S(1)}, f32[32,64,1]{1,0,2:T(8,128)S(1)}, u32[]{:S(2)}, u32[]{:S(2)}) collective-permute-start(f32[32,64,1]{1,0,2:T(8,128)S(1)} %copy.63), channel_id=1, source_target_pairs={{1,0},{2,1},{3,2},{4,3},{5,4},{6,5},{7,6},{0,7},{9,8},{10,9},{11,1... | collective-permute-start | bytes 24584 | tf_op jit(solution)/shard_map/ppermute | solution.py:25
  47.6 1.4 copy.66
  49.0 2.3 fusion.43
  51.3 4.9 %collective-permute-start.8 = (f32[32,1,128]{2,1,0:T(1,128)S(1)}, f32[32,1,128]{2,1,0:T(1,128)S(1)}, u32[]{:S(2)}, u32[]{:S(2)}) collective-permute-start(f32[32,1,128]{2,1,0:T(1,128)S(1)} %get-tuple-element.14), channel_id=1, source_target_pairs={{8,0},{16,8},{24,16},{32,24},{40,32},{48,40},{56,48},{64,56},{72,6... | collective-permute-start | bytes 49160 | tf_op jit(solution)/shard_map/ppermute | solution.py:25
  56.2 1.9 collective-permute-start.9
  58.9 3.5 collective-permute-start.10
  63.9 1.4 copy.70
  65.3 2.3 fusion.31
  67.7 4.9 %collective-permute-start.12 = (f32[32,1,128]{2,1,0:T(1,128)S(1)}, f32[32,1,128]{2,1,0:T(1,128)S(1)}, u32[]{:S(2)}, u32[]{:S(2)}) collective-permute-start(f32[32,1,128]{2,1,0:T(1,128)S(1)} %get-tuple-element.10), channel_id=1, source_target_pairs={{8,0},{16,8},{24,16},{32,24},{40,32},{48,40},{56,48},{64,56},{72,6... | collective-permute-start | bytes 49160 | tf_op jit(solution)/shard_map/ppermute | solution.py:25
  72.5 1.9 collective-permute-start.13
  75.2 3.5 collective-permute-start.14
  80.7 1.1 fusion.19
  81.8 1.6 copy.75
  83.4 10.8 %all-to-all-start = ((f32[64,32,1,128]{3,1,2,0:T(8,128)}), f32[64,32,1,128]{3,1,2,0:T(8,128)S(1)}, u32[]{:S(2)}, u32[]{:S(2)}) async-start(f32[64,32,1,128]{3,1,2,0:T(8,128)} %copy.75), calls=%async_computation | async-start | bytes 2097152 | tf_op jit(solution)/shard_map/all_to_all | solution.py:53
  95.1 1.3 dynamic-slice.2
  96.4 1.3 dynamic-slice
  99.7 22.7 %all-to-all-done = f32[64,32,1,128]{3,1,2,0:T(8,128)S(1)} async-done(((f32[64,32,1,128]{3,1,2,0:T(8,128)}), f32[64,32,1,128]{3,1,2,0:T(8,128)S(1)}, u32[]{:S(2)}, u32[]{:S(2)}) %all-to-all-start) | async-done | bytes 1048608 | tf_op jit(solution)/shard_map/all_to_all | solution.py:53
  122.8 5.0 %gather_fusion = f32[1024,256]{1,0:T(8,128)S(1)} fusion(f32[256,1,1024]{0,2,1:T(8,128)S(1)} %bitcast.138, s32[1024]{0:T(1024)S(1)} %bitcast.139), kind=kCustom, calls=%fused_computation | custom fusion | bytes 2105344 | tf_op jit(solution)/shard_map/gather | solution.py:157
  128.1 2.3 fusion
  130.5 0.9 copy.78
  132.8 13.9 %fusion.72 = f32[1,8,4,2,4]{4,0,3,2,1:T(1,128)S(1)} fusion(f32[8,4,2,4,1024]{4,3,2,1,0:T(4,128)S(1)} %mul.210, f32[1,1024]{1,0:T(1,128)S(1)} %copy-done.5, f32[1,1024]{1,0:T(1,128)S(1)} %bitcast.154), kind=kOutput, calls=%fused_computation.137 | convolution fusion | flops 3146752 | bytes 1057792 | tf_op jit(solution)/shard_map/dot_general | solution.py:163
  147.7 3.7 %reduce-scatter.4.cloned.1.call-done = f32[16,4,256]{2,0,1:T(8,128)} async-done(((f32[64,4,256]{2,0,1:T(8,128)}), f32[16,4,256]{2,0,1:T(8,128)}) %reduce-scatter.4.cloned.1.call-update) | async-done | bytes 65552 | tf_op jit(solution)/shard_map/reduce_scatter | solution.py:68
  152.0 30.6 %reduce-scatter.8.cloned.1.call-done = f32[16,4]{1,0:T(8,128)} async-done(((f32[64,4]{1,0:T(8,128)}), f32[16,4]{1,0:T(8,128)}) %reduce-scatter.8.cloned.1.call-update) | async-done | bytes 272 | tf_op jit(solution)/shard_map/reduce_scatter | solution.py:68
  182.6 5.0 %all-reduce.9 = f32[16,4]{1,0:T(8,128)S(1)} all-reduce(f32[16,4]{1,0:T(8,128)} %reduce-scatter.8.cloned.1.call-done), channel_id=10, replica_groups=mesh['member'=8,'domain'=12,'role_0'=4,'role_1'=2] {'role_1'}, use_global_device_ids=true, to_apply=%region_6.7.clone | all-reduce | flops 64 | bytes 512
  187.6 20.6 %reduce-scatter.6.cloned.1.call-done = f32[8,4,256]{2,0,1:T(8,128)} async-done(((f32[16,4,256]{2,0,1:T(8,128)}), f32[8,4,256]{2,0,1:T(8,128)}) %reduce-scatter.6.cloned.1.call-update) | async-done | bytes 32784 | tf_op jit(solution)/shard_map/reduce_scatter | solution.py:68
  208.2 0.8 copy.79
  209.0 21.1 %all-reduce.11 = (f32[8,4,256]{2,1,0:T(4,128)S(1)}, f32[8,4]{1,0:T(8,128)S(1)}) all-reduce(f32[8,4,256]{2,1,0:T(4,128)S(1)} %copy.79, f32[8,4]{1,0:T(8,128)S(1)} %constant_dynamic-slice_fusion.1), channel_id=8, replica_groups=mesh['member'=8,'domain'=12,'role_0'=4,'role_1'=2] {'member'}, use_global_device_ids=true, to_apply=%region_3.4.clone | all-reduce | flops 8224 | bytes 65792
  230.8 18.3 %all_gather.30 = f32[8,4,256]{2,1,0:T(4,128)S(1)} all-gather(f32[1,4,256]{2,1,0:T(4,128)S(1)} %constant_dynamic-slice_fusion.2), channel_id=1, replica_groups=mesh['member'=8,'domain'=12,'role_0'=4,'role_1'=2] {'member'}, dimensions={0}, use_global_device_ids=true | all-gather | bytes 36864 | tf_op jit(solution)/shard_map/all_gather | solution.py:75
  249.1 15.2 %all-gather = f32[16,4,256]{2,0,1:T(8,128)S(1)} all-gather(f32[8,4,256]{2,0,1:T(8,128)S(1)} %copy.80), channel_id=2, replica_groups=mesh['member'=8,'domain'=12,'role_0'=4,'role_1'=2] {'role_1'}, dimensions={0}, use_global_device_ids=true | all-gather | bytes 98304 | tf_op jit(solution)/shard_map/all_gather | solution.py:75
  264.3 10.2 %all-gather.1 = f32[8,8,4,256]{3,1,0,2:T(8,128)S(1)} all-gather(f32[2,8,4,256]{3,1,0,2:T(8,128)S(1)} %bitcast.151), channel_id=3, replica_groups=mesh['member'=8,'domain'=12,'role_0'=4,'role_1'=2] {'role_0'}, dimensions={0}, use_global_device_ids=true | all-gather | bytes 327680 | tf_op jit(solution)/shard_map/all_gather | solution.py:75
  274.8 0.9 multiply_reduce_fusion
  283.6 10.7 %all-gather.4 = f32[8,1,4]{2,1,0:T(1,128)S(1)} all-gather(f32[1,1,4]{2,1,0:T(1,128)S(1)} %fusion.75), channel_id=1, replica_groups=mesh['member'=8,'domain'=12,'role_0'=4,'role_1'=2] {'member'}, dimensions={0}, use_global_device_ids=true | all-gather | bytes 144 | tf_op jit(solution)/shard_map/all_gather | solution.py:75
  294.4 7.9 %all-gather.5 = f32[2,8,4]{1,2,0:T(4,128)S(1)} all-gather(f32[1,8,4]{1,2,0:T(4,128)S(1)} %bitcast.158), channel_id=4, replica_groups=mesh['member'=8,'domain'=12,'role_0'=4,'role_1'=2] {'role_1'}, dimensions={0}, use_global_device_ids=true | all-gather | bytes 384 | tf_op jit(solution)/shard_map/all_gather | solution.py:75
  302.3 9.1 %all-gather.3 = f32[8,8,4]{1,2,0:T(4,128)S(1)} all-gather(f32[2,8,4]{1,2,0:T(4,128)S(1)} %all-gather.5), channel_id=5, replica_groups=mesh['member'=8,'domain'=12,'role_0'=4,'role_1'=2] {'role_0'}, dimensions={0}, use_global_device_ids=true | all-gather | bytes 1280 | tf_op jit(solution)/shard_map/all_gather | solution.py:75
  312.4 1.2 fusion.2
  314.0 38.7 %all_to_all.10 = f32[64,32,1,128]{3,1,2,0:T(8,128)S(1)} all-to-all(f32[64,32,1,128]{3,1,2,0:T(8,128)S(1)} %bitcast.145), channel_id=1, replica_groups=mesh['member'=8,'domain'=12,'role_0'=4,'role_1'=2] {'member','role_0','r..., dimensions={0} | all-to-all | bytes 2097152 | tf_op jit(solution)/shard_map/all_to_all | solution.py:53
  352.7 1.6 copy.103
  (103 shorter events, 23.2 us)
Async XLA Ops:
  7.5 24.8 %collective-permute-start = (f32[32,1,128]{2,1,0:T(1,128)S(1)}, f32[32,1,128]{2,1,0:T(1,128)S(1)}, u32[]{:S(2)}, u32[]{:S(2)}) collective-permute-start(f32[32,1,128]{2,1,0:T(1,128)S(1)} %get-tuple-element.22), channel_id=1, source_target_pairs={{8,0},{16,8},{24,16},{32,24},{40,32},{48,40},{56,48},{64,56},{72,6... | collective-permute-start | bytes 49160 | tf_op jit(solution)/shard_map/ppermute | solution.py:25
  22.7 9.7 %collective-permute-start.1 = (f32[32,1,128]{2,1,0:T(1,128)S(1)}, f32[32,1,128]{2,1,0:T(1,128)S(1)}, u32[]{:S(2)}, u32[]{:S(2)}) collective-permute-start(f32[32,1,128]{2,1,0:T(1,128)S(1)} %get-tuple-element.21), channel_id=1, source_target_pairs={{0,8},{8,16},{16,24},{24,32},{32,40},{40,48},{48,56},{56,64},{64,7... | collective-permute-start | bytes 49160 | tf_op jit(solution)/shard_map/ppermute | solution.py:24
  27.0 3.5 collective-permute-start.2
  28.4 4.0 %copy-start = (f32[32,64,128]{2,1,0:T(8,128)S(1)}, f32[32,64,128]{2,1,0:T(8,128)}, u32[]{:S(2)}) copy-start(f32[32,64,128]{2,1,0:T(8,128)} %param.8) | copy-start | bytes 3145732
  28.4 2.6 collective-permute-start.3
  30.9 1.5 copy-start.1
  30.9 1.4 copy-start.2
  30.9 1.4 copy-start.3
  34.8 14.2 %collective-permute-start.4 = (f32[32,1,128]{2,1,0:T(1,128)S(1)}, f32[32,1,128]{2,1,0:T(1,128)S(1)}, u32[]{:S(2)}, u32[]{:S(2)}) collective-permute-start(f32[32,1,128]{2,1,0:T(1,128)S(1)} %get-tuple-element.18), channel_id=1, source_target_pairs={{8,0},{16,8},{24,16},{32,24},{40,32},{48,40},{56,48},{64,56},{72,6... | collective-permute-start | bytes 49160 | tf_op jit(solution)/shard_map/ppermute | solution.py:25
  39.6 9.4 %collective-permute-start.5 = (f32[32,1,128]{2,1,0:T(1,128)S(1)}, f32[32,1,128]{2,1,0:T(1,128)S(1)}, u32[]{:S(2)}, u32[]{:S(2)}) collective-permute-start(f32[32,1,128]{2,1,0:T(1,128)S(1)} %get-tuple-element.17), channel_id=1, source_target_pairs={{0,8},{8,16},{16,24},{24,32},{32,40},{40,48},{48,56},{56,64},{64,7... | collective-permute-start | bytes 49160 | tf_op jit(solution)/shard_map/ppermute | solution.py:24
  42.3 4.6 %collective-permute-start.6 = (f32[32,64,1]{1,0,2:T(8,128)S(1)}, f32[32,64,1]{1,0,2:T(8,128)S(1)}, u32[]{:S(2)}, u32[]{:S(2)}) collective-permute-start(f32[32,64,1]{1,0,2:T(8,128)S(1)} %copy.63), channel_id=1, source_target_pairs={{1,0},{2,1},{3,2},{4,3},{5,4},{6,5},{7,6},{0,7},{9,8},{10,9},{11,1... | collective-permute-start | bytes 24584 | tf_op jit(solution)/shard_map/ppermute | solution.py:25
  46.4 1.2 collective-permute-start.7
  51.3 14.0 %collective-permute-start.8 = (f32[32,1,128]{2,1,0:T(1,128)S(1)}, f32[32,1,128]{2,1,0:T(1,128)S(1)}, u32[]{:S(2)}, u32[]{:S(2)}) collective-permute-start(f32[32,1,128]{2,1,0:T(1,128)S(1)} %get-tuple-element.14), channel_id=1, source_target_pairs={{8,0},{16,8},{24,16},{32,24},{40,32},{48,40},{56,48},{64,56},{72,6... | collective-permute-start | bytes 49160 | tf_op jit(solution)/shard_map/ppermute | solution.py:25
  56.2 9.1 %collective-permute-start.9 = (f32[32,1,128]{2,1,0:T(1,128)S(1)}, f32[32,1,128]{2,1,0:T(1,128)S(1)}, u32[]{:S(2)}, u32[]{:S(2)}) collective-permute-start(f32[32,1,128]{2,1,0:T(1,128)S(1)} %get-tuple-element.13), channel_id=1, source_target_pairs={{0,8},{8,16},{16,24},{24,32},{32,40},{40,48},{48,56},{56,64},{64,7... | collective-permute-start | bytes 49160 | tf_op jit(solution)/shard_map/ppermute | solution.py:24
  58.9 4.3 %collective-permute-start.10 = (f32[32,64,1]{1,0,2:T(8,128)S(1)}, f32[32,64,1]{1,0,2:T(8,128)S(1)}, u32[]{:S(2)}, u32[]{:S(2)}) collective-permute-start(f32[32,64,1]{1,0,2:T(8,128)S(1)} %copy.67), channel_id=1, source_target_pairs={{1,0},{2,1},{3,2},{4,3},{5,4},{6,5},{7,6},{0,7},{9,8},{10,9},{11,1... | collective-permute-start | bytes 24584 | tf_op jit(solution)/shard_map/ppermute | solution.py:25
  62.7 1.2 collective-permute-start.11
  67.7 13.0 %collective-permute-start.12 = (f32[32,1,128]{2,1,0:T(1,128)S(1)}, f32[32,1,128]{2,1,0:T(1,128)S(1)}, u32[]{:S(2)}, u32[]{:S(2)}) collective-permute-start(f32[32,1,128]{2,1,0:T(1,128)S(1)} %get-tuple-element.10), channel_id=1, source_target_pairs={{8,0},{16,8},{24,16},{32,24},{40,32},{48,40},{56,48},{64,56},{72,6... | collective-permute-start | bytes 49160 | tf_op jit(solution)/shard_map/ppermute | solution.py:25
  72.5 8.2 %collective-permute-start.13 = (f32[32,1,128]{2,1,0:T(1,128)S(1)}, f32[32,1,128]{2,1,0:T(1,128)S(1)}, u32[]{:S(2)}, u32[]{:S(2)}) collective-permute-start(f32[32,1,128]{2,1,0:T(1,128)S(1)} %get-tuple-element.9), channel_id=1, source_target_pairs={{0,8},{8,16},{16,24},{24,32},{32,40},{40,48},{48,56},{56,64},{64,7... | collective-permute-start | bytes 49160 | tf_op jit(solution)/shard_map/ppermute | solution.py:24
  75.2 4.3 %collective-permute-start.14 = (f32[32,64,1]{1,0,2:T(8,128)S(1)}, f32[32,64,1]{1,0,2:T(8,128)S(1)}, u32[]{:S(2)}, u32[]{:S(2)}) collective-permute-start(f32[32,64,1]{1,0,2:T(8,128)S(1)} %copy.71), channel_id=1, source_target_pairs={{1,0},{2,1},{3,2},{4,3},{5,4},{6,5},{7,6},{0,7},{9,8},{10,9},{11,1... | collective-permute-start | bytes 24584 | tf_op jit(solution)/shard_map/ppermute | solution.py:25
  79.1 1.2 collective-permute-start.15
  83.4 39.0 %all-to-all-start = ((f32[64,32,1,128]{3,1,2,0:T(8,128)}), f32[64,32,1,128]{3,1,2,0:T(8,128)S(1)}, u32[]{:S(2)}, u32[]{:S(2)}) async-start(f32[64,32,1,128]{3,1,2,0:T(8,128)} %copy.75), calls=%async_computation | async-start | bytes 2097152 | tf_op jit(solution)/shard_map/all_to_all | solution.py:53
  94.3 57.1 %reduce-scatter.4.cloned.1.call-start = ((), (), s32[]{:S(2)}) async-start(), calls=%async_computation.5 | async-start | bytes 327680 | tf_op jit(solution)/shard_map/reduce_scatter | solution.py:68
  98.3 0.7 copy-start.4
  99.0 0.7 copy-start.6
  131.4 51.2 %reduce-scatter.8.cloned.1.call-start = ((), (), s32[]{:S(2)}) async-start(), calls=%async_computation.7 | async-start | bytes 40960 | tf_op jit(solution)/shard_map/reduce_scatter | solution.py:68
  132.1 0.7 copy-start.5
  147.3 60.9 %reduce-scatter.6.cloned.1.call-start = ((), (), s32[]{:S(2)}) async-start(), calls=%async_computation.6 | async-start | bytes 98304 | tf_op jit(solution)/shard_map/reduce_scatter | solution.py:68
Sparse Core Ops, SparseCore 0:
  131.5 19.7 reduce-scatter.3
  154.4 28.1 reduce-scatter.7
  185.6 22.5 reduce-scatter.5
where the time goes:
time: 362 us; the launch traced here: 361 us
  blocking collectives  136 us (38%)
  waiting for transfers between devices  81 us (22%)
  starting transfers between devices  61.5 us (17%)
  local copies, waits for them, and re-layouts  32.2 us (9%)
  matrix products  24.2 us (7%)
  between operations  15.8 us (4%)
  other arithmetic  9.69 us (3%)
    all_gather x6, blocking collectives, stacked_from(): parts = lax.all_gather(parts, axes[k])  71.6 us
    reduce_scatter x3, waiting for transfers between devices, sum_in_order(): parts = lax.psum_scatter(parts, axes[k], scatter_dimension=0, tiled=True)  54.8 us
    ppermute x8, starting transfers between devices, with_halo(): lax.ppermute(initial, axis, [(b, a) for a, b in up])  41.4 us
    all_to_all x1, blocking collectives, joined_exchange(): parts = lax.all_to_all(parts, axis, split_axis=0, concat_axis=0, tiled=True)  38.7 us
    unnamed x2, blocking collectives  26.1 us
    all_to_all x1, waiting for transfers between devices, joined_exchange(): parts = lax.all_to_all(parts, axis, split_axis=0, concat_axis=0, tiled=True)  22.7 us
    dot_general x1, matrix products, shards(): jnp.dot(weighted, values - centre_obs, precision=precise)  13.9 us
    all_to_all x1, starting transfers between devices, joined_exchange(): parts = lax.all_to_all(parts, axis, split_axis=0, concat_axis=0, tiled=True)  10.8 us
  transfers between devices with their start and end apart: 20, of which 11 were waited for; matrix products, arithmetic and copies ran while one was open for 9% of the time, Pallas kernels for 0%

commit v1 on v0

v1 whole, which is shorter than its diff:
```python
import functools

import jax
import jax.numpy as jnp
from jax import lax
from jax.experimental import pallas as pl
from jax.experimental.pallas import tpu as pltpu
from jax.sharding import PartitionSpec as P

STEPS = 4
ITERS = 6
LANES = 128
GROUP = 8
SEG = 24
F32 = jnp.float32
BF16 = jnp.bfloat16
MESH = pl.DeviceIdType.MESH
NN = (((1,), (0,)), ((), ()))
NT = (((1,), (1,)), ((), ()))


def halves(a):
    high = a.astype(BF16)
    return high, (a - high.astype(F32)).astype(BF16)


def product(a, b, dims=NN):
    (ah, al), (bh, bl) = a, b
    dot = functools.partial(lax.dot_general, dimension_numbers=dims, preferred_element_type=F32)
    return dot(ah, bh) + (dot(ah, bl) + dot(al, bh))


def kernel(
    sizes,
    count_ref,
    fields_ref,
    cells_ref,
    values_ref,
    weights_ref,
    out_ref,
    field_a,
    field_b,
    strip_a,
    strip_b,
    strip_coef,
    pack_right,
    pack_left,
    halo_left,
    halo_right,
    final,
    received,
    obs_part,
    obs_role,
    obs_own,
    obs_all,
    gram_part,
    gram_role,
    gram_own,
    gram,
    current,
    inverse,
    mixing,
    dev_high,
    dev_low,
    centre_buf,
    result,
    load_sem,
    halo_send,
    halo_recv,
    peer_send,
    peer_recv,
):
    n_member, n_domain, n_role, members = sizes
    rows = 64
    chunk = rows // n_member
    total = members * n_member
    slot_groups = 8 // n_role
    gram_rows = total // n_role
    groups = members // GROUP
    me_m = lax.axis_index("member")
    me_d = lax.axis_index("domain")
    me_r = lax.axis_index("role")

    def other(me, step, n):
        return lax.rem(me + (step + n), n)

    down, up = other(me_d, 1, n_domain), other(me_d, -1, n_domain)
    right, left = other(me_r, 1, n_role), other(me_r, -1, n_role)

    load = pltpu.make_async_copy(fields_ref, field_a.at[4 : 4 + rows], load_sem.at[0])
    load.start()

    barrier = pltpu.get_barrier_semaphore()
    greeted = 0
    for d in (down, up):
        for r in (me_r, right, left):
            pl.semaphore_signal(barrier, inc=1, device_id={"domain": d, "role": r}, device_id_type=MESH)
            greeted += 1
    for step in range(1, n_role):
        pl.semaphore_signal(barrier, inc=1, device_id={"role": other(me_r, step, n_role)}, device_id_type=MESH)
        greeted += 1
    for step in range(1, n_member):
        pl.semaphore_signal(barrier, inc=1, device_id={"member": other(me_m, step, n_member)}, device_id_type=MESH)
        greeted += 1

    lane = lax.broadcasted_iota(jnp.int32, (GROUP, LANES), 1)
    seg_lane = lane
    for s in range(1, 6):
        seg_lane = jnp.where(lane >= SEG * s, lane - SEG * s, seg_lane)

    def own_strip(row):
        strip = jnp.zeros((GROUP, LANES), F32)
        for s in range(groups + 1):
            block = field_a[row, GROUP * s : GROUP * (s + 1), :]
            base = SEG * s
            ends = pltpu.roll(block, (base + 8) % LANES, 1)
            starts = pltpu.roll(block, (base + 16) % LANES, 1)
            strip = jnp.where((lane >= base) & (lane < base + 8), ends, strip)
            strip = jnp.where((lane >= base + 16) & (lane < base + 24), starts, strip)
        return strip

    load.wait()

    def pack(q, carry):
        to_right = to_left = jnp.zeros((GROUP, LANES), F32)
        for t in range(4):
            row = 4 + 4 * q + t
            strip = own_strip(row)
            strip_a[row] = strip
            low, high = 4 + 4 * t, 16 - 4 * t
            moved = pltpu.roll(strip, 4 * t, 1) if t else strip
            to_right = jnp.where((seg_lane >= low) & (seg_lane < low + 4), moved, to_right)
            moved = pltpu.roll(strip, LANES - 4 * t, 1) if t else strip
            to_left = jnp.where((seg_lane >= high) & (seg_lane < high + 4), moved, to_left)
        pack_right[q] = to_right
        pack_left[q] = to_left
        return carry

    pl.semaphore_wait(barrier, greeted)

    def halo_copy(k, src, dst, where):
        return pltpu.make_async_remote_copy(
            src_ref=src, dst_ref=dst, send_sem=halo_send.at[k], recv_sem=halo_recv.at[k],
            device_id=where, device_id_type=MESH,
        )

    quads = rows // 4
    row_halos = [
        halo_copy(0, fields_ref.at[rows - 4 : rows], field_a.at[0:4], {"domain": down}),
        halo_copy(1, fields_ref.at[0:4], field_a.at[rows + 4 : rows + 8], {"domain": up}),
    ]
    for copy in row_halos:
        copy.start()
    lax.fori_loop(0, quads, pack, 0, unroll=2)
    col_halos = [
        halo_copy(4, pack_right.at[quads - 1], halo_left.at[0], {"domain": down, "role": right}),
        halo_copy(5, pack_right.at[0], halo_left.at[quads + 1], {"domain": up, "role": right}),
        halo_copy(6, pack_left.at[quads - 1], halo_right.at[0], {"domain": down, "role": left}),
        halo_copy(7, pack_left.at[0], halo_right.at[quads + 1], {"domain": up, "role": left}),
        halo_copy(2, pack_right, halo_left.at[1 : quads + 1], {"role": right}),
        halo_copy(3, pack_left, halo_right.at[1 : quads + 1], {"role": left}),
    ]
    for copy in col_halos:
        copy.start()
    for copy in row_halos:
        copy.wait()
    for t in range(4):
        strip_a[t] = own_strip(t)
        strip_a[rows + 4 + t] = own_strip(rows + 4 + t)
    for copy in col_halos:
        copy.wait()

    def unpack(q, carry):
        from_left = halo_left[q]
        from_right = halo_right[q]
        for t in range(4):
            row = 4 * q + t
            strip = strip_a[row]
            moved = pltpu.roll(from_left, (8 - 4 * t) % LANES, 1) if t != 2 else from_left
            strip = jnp.where((seg_lane >= 12) & (seg_lane < 16), moved, strip)
            moved = pltpu.roll(from_right, (4 * t - 8) % LANES, 1) if t != 2 else from_right
            strip = jnp.where((seg_lane >= 8) & (seg_lane < 12), moved, strip)
            strip_a[row] = strip
            coef = strip
            for s in range(groups):
                moved = pltpu.roll(strip, (SEG * (s - groups)) % LANES, 1)
                coef = jnp.where((lane >= SEG * s) & (lane < SEG * (s + 1)), moved, coef)
            strip_coef[row] = coef
        return carry

    lax.fori_loop(0, quads + 2, unpack, 0, unroll=2)

    def advanced(now, before, after, coef):
        return (
            now * coef[0]
            + (after + pltpu.roll(now, LANES - 1, 1)) * coef[1]
            + before * coef[2]
            + pltpu.roll(now, 1, 1) * coef[3]
        )

    def field_coef(row):
        return [field_a[row, members + k : members + k + 1, :] for k in range(4)]

    def seam_coef(row):
        return [strip_coef[row, k : k + 1, :] for k in range(4)]

    def step_rows(source, target, strip_source, strip_target, first, amount):
        before = source[first - 1, :members, :]
        now = source[first, :members, :]
        seam_before = strip_source[first - 1]
        seam_now = strip_source[first]
        for i in range(amount):
            row = first + i
            after = source[row + 1, :members, :]
            seam_after = strip_source[row + 1]
            target[row, :members, :] = advanced(now, before, after, field_coef(row))
            strip_target[row] = advanced(seam_now, seam_before, seam_after, seam_coef(row))
            before, now = now, after
            seam_before, seam_now = seam_now, seam_after

    pairs = ((field_a, field_b, strip_a, strip_b), (field_b, field_a, strip_b, strip_a))
    for step in range(STEPS - 1):

        def body(i, carry, refs=pairs[step % 2]):
            step_rows(*refs, 1 + 10 * i, 10)
            return carry

        lax.fori_loop(0, 7, body, 0)

    source, _, strip_source, _ = pairs[(STEPS - 1) % 2]

    def last_rows(first, amount):
        before = source[first - 1, :members, :]
        now = source[first, :members, :]
        seam_before = strip_source[first - 1]
        seam_now = strip_source[first]
        for i in range(amount):
            row = first + i
            after = source[row + 1, :members, :]
            seam_after = strip_source[row + 1]
            new = advanced(now, before, after, field_coef(row))
            seam = advanced(seam_now, seam_before, seam_after, seam_coef(row))
            for s in range(groups):
                begin = pltpu.roll(seam, (-(SEG * s + 16)) % LANES, 1)
                end = pltpu.roll(seam, (120 - SEG * s) % LANES, 1)
                block = new[GROUP * s : GROUP * (s + 1), :]
                block = jnp.where(lane < 4, begin, jnp.where(lane >= LANES - 4, end, block))
                final[row - 4, GROUP * s : GROUP * (s + 1), :] = block
            before, now = now, after
            seam_before, seam_now = seam_now, seam_after

    def last_body(i, carry):
        last_rows(4 + 8 * i, 8)
        return carry

    lax.fori_loop(0, rows // 8, last_body, 0)

    def peer_copy(stage, step, src, dst, axis):
        me, n = (me_m, n_member) if axis == "member" else (me_r, n_role)
        return pltpu.make_async_remote_copy(
            src_ref=src, dst_ref=dst, send_sem=peer_send.at[stage, step], recv_sem=peer_recv.at[stage, step],
            device_id={axis: other(me, step, n)}, device_id_type=MESH,
        )

    order = sorted(range(1, n_member), key=lambda s: -min(s, n_member - s))
    forward = []
    for step in order:
        first = pl.multiple_of(chunk * other(me_m, step, n_member), chunk)
        forward.append(
            peer_copy(
                0, step, final.at[pl.ds(first, chunk)],
                received.at[:, pl.ds(pl.multiple_of(members * me_m, members), members), :], "member",
            )
        )
    keep = pltpu.make_async_copy(
        final.at[pl.ds(pl.multiple_of(chunk * me_m, chunk), chunk)],
        received.at[:, pl.ds(pl.multiple_of(members * me_m, members), members), :],
        load_sem.at[1],
    )
    early = 2
    for copy in forward[:early]:
        copy.start()

    def observe(g, carry):
        cell = cells_ref[pl.ds(g, 1), :]
        here = ((cell // LANES) % n_role) == me_r
        row_of = jnp.where(here, cell // (LANES * n_role), -1)
        row_of = jnp.broadcast_to(row_of, (members, LANES))
        col_of = jnp.broadcast_to(cell % LANES, (members, LANES))

        def some(q, seen):
            for t in range(16):
                row = 16 * q + t
                picked = jnp.take_along_axis(final[row], col_of, axis=1, mode="promise_in_bounds")
                seen = jnp.where(row_of == row, picked, seen)
            return seen

        obs_part[g] = lax.fori_loop(0, rows // 16, some, jnp.zeros((members, LANES), F32))
        return carry

    lax.fori_loop(0, 8, observe, 0)

    def own_groups(r):
        return pl.ds(slot_groups * r, slot_groups)

    copies = []
    for step in range(1, n_role):
        copies.append(
            peer_copy(1, step, obs_part.at[own_groups(other(me_r, step, n_role))], obs_role.at[me_r], "role")
        )
        copies[-1].start()
    obs_role[me_r] = obs_part[own_groups(me_r)]
    for copy in copies:
        copy.wait()
    obs_own[...] = functools.reduce(jnp.add, [obs_role[r] for r in range(n_role)])

    mine = pl.ds(pl.multiple_of(members * me_m, members), members)
    copies = []
    for step in order:
        copies.append(peer_copy(2, step, obs_own, obs_all.at[:, mine, :], "member"))
        copies[-1].start()
    for copy in forward[early:]:
        copy.start()
    keep.start()
    obs_all[:, mine, :] = obs_own[...]
    for copy in copies:
        copy.wait()

    part = jnp.zeros((total, total), F32)
    push = jnp.zeros((GROUP, total), F32)
    slot = lax.broadcasted_iota(jnp.int32, (1, LANES), 1)
    for g in range(slot_groups):
        place = slot_groups * me_r + g
        observed = obs_all[g]
        centre = jnp.sum(observed, axis=0, keepdims=True) * (1.0 / total)
        deviation = observed - centre
        usable = slot + place * LANES < count_ref[0]
        weighted = deviation * jnp.where(usable, weights_ref[pl.ds(place, 1), :], 0.0)
        gap = jnp.broadcast_to(values_ref[pl.ds(place, 1), :] - centre, (GROUP, LANES))
        weighted = halves(weighted)
        part = part + product(halves(deviation), weighted, NT)
        push = push + product(halves(gap), weighted, NT)
    for r in range(n_role):
        gram_part[r, :gram_rows, :] = part[gram_rows * r : gram_rows * (r + 1), :]
        gram_part[r, gram_rows:, :] = push

    copies = []
    for step in range(1, n_role):
        copies.append(
            peer_copy(3, step, gram_part.at[other(me_r, step, n_role)], gram_role.at[me_r], "role")
        )
        copies[-1].start()
    gram_role[me_r] = gram_part[me_r]
    for copy in copies:
        copy.wait()
    summed = functools.reduce(jnp.add, [gram_role[r] for r in range(n_role)])
    innovation = summed[gram_rows:, :]
    gram_own[...] = summed[:gram_rows, :]
    band = pl.ds(pl.multiple_of(gram_rows * me_r, gram_rows), gram_rows)
    copies = []
    for step in range(1, n_role):
        copies.append(peer_copy(4, step, gram_own, gram.at[band, :], "role"))
        copies[-1].start()
    gram[band, :] = gram_own[...]
    for copy in copies:
        copy.wait()

    across = lax.broadcasted_iota(jnp.int32, (total, total), 1)
    along = lax.broadcasted_iota(jnp.int32, (total, total), 0)
    diagonal = across == along
    matrix = gram[...] + jnp.where(diagonal, total - 1.0, 0.0)
    squares = jnp.sum(jnp.sum(matrix * matrix, axis=0, keepdims=True), axis=1, keepdims=True)
    scaling = jnp.sqrt(squares)
    scaled = matrix / scaling
    middle = jnp.where(diagonal, 1.5, 0.0) - 0.5 * scaled
    current[...] = product(halves(scaled), halves(middle))
    inverse[...] = middle

    def newton(i, carry):
        cur, inv = halves(current[...]), halves(inverse[...])
        mid = halves(jnp.where(diagonal, 1.5, 0.0) - 0.5 * product(inv, cur))
        current[...] = product(cur, mid)
        inverse[...] = product(mid, inv)
        return carry

    lax.fori_loop(0, ITERS - 2, newton, 0)
    inv = halves(inverse[...])
    mid = halves(jnp.where(diagonal, 1.5, 0.0) - 0.5 * product(inv, halves(current[...])))
    root = product(mid, inv)
    root_halves = halves(root)
    shifted = product(halves(product(halves(innovation), root_halves)), root_halves) / scaling
    mixing[...] = root * jnp.sqrt((total - 1.0) / scaling) + shifted[0:1, :]

    for copy in forward:
        copy.wait()
    keep.wait()
    for i in range(chunk):
        block = received[i]
        centre = jnp.sum(block, axis=0, keepdims=True) * (1.0 / total)
        high, low = halves(block - centre)
        span = slice(LANES * i, LANES * (i + 1))
        dev_high[:, span] = high
        dev_low[:, span] = low
        centre_buf[:, span] = centre

    back = []
    target_rows = pl.ds(pl.multiple_of(chunk * me_m, chunk), chunk)
    for step in order + [0]:
        first = pl.multiple_of(members * other(me_m, step, n_member), members)
        share = halves(mixing[pl.ds(first, members), :])
        updated = product(share, (dev_high[...], dev_low[...])) + centre_buf[...]
        for i in range(chunk):
            result[step, i] = updated[:, LANES * i : LANES * (i + 1)]
        if step:
            copy = peer_copy(5, step, result.at[step], out_ref.at[target_rows], "member")
        else:
            copy = pltpu.make_async_copy(result.at[step], out_ref.at[target_rows], load_sem.at[2])
        copy.start()
        back.append(copy)
    for copy in back:
        copy.wait()


def shards(sizes, ensemble, diffusion, drift_rows, drift_cols, cells, count, values, weights):
    n_member, n_domain, n_role = sizes
    members, rows, cols = ensemble.shape
    total = members * n_member
    coef = jnp.stack(
        [
            1.0 - 4.0 * diffusion - drift_rows - drift_cols,
            diffusion,
            diffusion + drift_rows,
            diffusion + drift_cols,
        ]
        + [jnp.zeros_like(diffusion)] * 4,
        axis=1,
    )
    fields = jnp.concatenate([jnp.transpose(ensemble, (1, 0, 2)), coef], axis=1)
    planes = members + GROUP
    chunk = rows // n_member
    slot_groups = 8 // n_role
    gram_rows = total // n_role

    def vmem(*shape, dtype=F32):
        return pltpu.VMEM(shape, dtype)

    packs = (rows // 4, GROUP, LANES)
    halos = (rows // 4 + 2, GROUP, LANES)
    out = pl.pallas_call(
        functools.partial(kernel, (n_member, n_domain, n_role, members)),
        name="forecast_analysis",
        out_shape=jax.ShapeDtypeStruct((rows, members, cols), F32),
        in_specs=[
            pl.BlockSpec(memory_space=pltpu.SMEM),
            pl.BlockSpec(memory_space=pl.ANY),
            pl.BlockSpec(memory_space=pltpu.VMEM),
            pl.BlockSpec(memory_space=pltpu.VMEM),
            pl.BlockSpec(memory_space=pltpu.VMEM),
        ],
        out_specs=pl.BlockSpec(memory_space=pl.ANY),
        scratch_shapes=[
            vmem(rows + 8, planes, cols),
            vmem(rows + 8, planes, cols),
            vmem(rows + 8, GROUP, LANES),
            vmem(rows + 8, GROUP, LANES),
            vmem(rows + 8, GROUP, LANES),
            vmem(*packs),
            vmem(*packs),
            vmem(*halos),
            vmem(*halos),
            vmem(rows, members, cols),
            vmem(chunk, total, cols),
            vmem(8, members, LANES),
            vmem(n_role, slot_groups, members, LANES),
            vmem(slot_groups, members, LANES),
            vmem(slot_groups, total, LANES),
            vmem(n_role, gram_rows + GROUP, total),
            vmem(n_role, gram_rows + GROUP, total),
            vmem(gram_rows, total),
            vmem(total, total),
            vmem(total, total),
            vmem(total, total),
            vmem(total, total),
            vmem(total, chunk * cols, dtype=BF16),
            vmem(total, chunk * cols, dtype=BF16),
            vmem(1, chunk * cols),
            vmem(n_member, chunk, members, cols),
            pltpu.SemaphoreType.DMA((3,)),
            pltpu.SemaphoreType.DMA((8,)),
            pltpu.SemaphoreType.DMA((8,)),
            pltpu.SemaphoreType.DMA((6, 8)),
            pltpu.SemaphoreType.DMA((6, 8)),
        ],
        compiler_params=pltpu.CompilerParams(
            collective_id=0, has_side_effects=True, vmem_limit_bytes=40 << 20
        ),
    )(
        count,
        fields,
        cells.reshape(8, LANES),
        values.reshape(8, LANES),
        weights.reshape(8, LANES),
    )
    return jnp.transpose(out, (1, 0, 2))


def solution(mesh):
    sizes = tuple(mesh.shape[a] for a in ("member", "domain", "role"))
    return jax.shard_map(
        functools.partial(shards, sizes),
        mesh=mesh,
        in_specs=(
            P("member", "domain", "role"),
            P("domain", "role"),
            P("domain", "role"),
            P("domain", "role"),
            P("domain", None),
            P("domain"),
            P("domain", None),
            P("domain", None),
        ),
        out_specs=P("member", "domain", "role"),
        check_vma=False,
    )
```

time: 362 us -> 98.8 us (0.27)
  blocking collectives: 136 us -> 0 us
  Pallas kernels: 0 us -> 93 us
  waiting for transfers between devices: 81 us -> 0 us
  starting transfers between devices: 61.5 us -> 0 us
  local copies, waits for them, and re-layouts: 32.2 us -> 3.93 us
  matrix products: 24.2 us -> 0 us
  between operations: 15.8 us -> 0.73 us
  other arithmetic: 9.69 us -> 0.84 us
    pallas_call x0 -> x1, Pallas kernels: none -> 93 us  [shards(): pl.pallas_call(functools.partial(kernel, (n_member, n_domain, n_role, mem...]
    all_gather x6 -> x0, blocking collectives: 71.6 us -> none  [stacked_from(): parts = lax.all_gather(parts, axes[k])]
    reduce_scatter x3 -> x0, waiting for transfers between devices: 54.8 us -> none  [sum_in_order(): parts = lax.psum_scatter(parts, axes[k], scatter_dimension=0, tiled=True)]
    ppermute x16 -> x0, starting transfers between devices: 50.2 us -> none  [the longest x8 41.4 us: with_halo(): lax.ppermute(initial, axis, [(b, a) for a, b in up])]
    all_to_all x1 -> x0, blocking collectives: 38.7 us -> none  [joined_exchange(): parts = lax.all_to_all(parts, axis, split_axis=0, concat_axis=0, tiled=True)]
    unnamed x2 -> x0, blocking collectives: 26.1 us -> none
    dot_general x22 -> x0, matrix products: 24.2 us -> none  [the longest x1 13.9 us: shards(): jnp.dot(weighted, values - centre_obs, precision=precise)]
    all_to_all x1 -> x0, waiting for transfers between devices: 22.7 us -> none  [joined_exchange(): parts = lax.all_to_all(parts, axis, split_axis=0, concat_axis=0, tiled=True)]
  transfers between devices with their start and end apart: 20 -> 0, of which waited for: 11 -> 0; matrix products, arithmetic and copies ran while one was open for 9% -> 0% of each run, Pallas kernels for 0% -> 0%
where the time goes in v1:
time: 98.8 us; the launch traced here: 98.5 us
  Pallas kernels  93 us (94%)
  local copies, waits for them, and re-layouts  3.93 us (4%)
    pallas_call x1, Pallas kernels, shards(): pl.pallas_call(functools.partial(kernel, (n_member, n_domain, n_role, mem...  93 us

profile of v1, /device:TPU:1, one launch (start us, length us, event | category | flops | bytes accessed | tf_op | source)
XLA Modules:
  0.0 98.5 jit_solution(16117263574520994779)
XLA Ops:
  0.0 0.0 copy-start.3
  0.0 0.8 fusion
  0.8 1.8 %copy.12 = f32[32,64,128]{2,0,1:T(8,128)S(1)} copy(f32[32,64,128]{2,1,0:T(8,128)} %param.8) | data formatting | bytes 2097152 | tf_op args[0]
  2.7 0.0 copy-done.3
  2.7 0.0 copy-start
  2.7 0.0 copy-start.1
  2.7 0.0 copy-start.2
  2.8 0.5 concatenate.7.fields_ref
  3.9 0.0 copy-done
  3.9 0.0 copy-done.1
  3.9 0.0 copy-done.2
  3.9 93.0 %forecast_analysis.1 = f32[64,32,128]{2,1,0:T(8,128)S(1)} custom-call(s32[1]{0:T(128)S(6)} %copy.13.count_ref, f32[64,40,128]{2,1,0:T(8,128)S(1)} %concatenate.7.fields_ref, s32[8,128]{1,0:T(8,128)S(1)} %bitcast.12, f32[8,128]{1,0:T(8,128)S(1)} %bitcast.13, f32[8,128]{1,0:T(8,128)S(1)} %bitcast.14), custom_call_target="tpu_custom_call" | custom-call | tf_op jit(solution)/shard_map/forecast_analysis/pallas_call | solution.py:449
  96.9 1.6 %copy.10 = f32[32,64,128]{2,1,0:T(8,128)} copy(f32[32,64,128]{2,0,1:T(8,128)S(1)} %bitcast.11) | data formatting | bytes 2097152 | tf_op jit(solution)/shard_map/transpose | solution.py:504
  (1 shorter events, 0.0 us)
Async XLA Ops:
  0.0 2.7 %copy-start.3 = (f32[64,128]{1,0:T(8,128)S(1)}, f32[64,128]{1,0:T(8,128)}, u32[]{:S(2)}) copy-start(f32[64,128]{1,0:T(8,128)} %param.9) | copy-start | bytes 98308
  2.7 1.2 %copy-start = (s32[1,1024]{1,0:T(1,128)S(1)}, s32[1,1024]{1,0:T(1,128)}, u32[]{:S(2)}) copy-start(s32[1,1024]{1,0:T(1,128)} %param.12) | copy-start | bytes 12292
  2.7 1.2 %copy-start.1 = (f32[1,1024]{1,0:T(1,128)S(1)}, f32[1,1024]{1,0:T(1,128)}, u32[]{:S(2)}) copy-start(f32[1,1024]{1,0:T(1,128)} %param.14) | copy-start | bytes 12292
  2.7 1.2 %copy-start.2 = (f32[1,1024]{1,0:T(1,128)S(1)}, f32[1,1024]{1,0:T(1,128)}, u32[]{:S(2)}) copy-start(f32[1,1024]{1,0:T(1,128)} %param.15) | copy-start | bytes 12292

commit v2 on v1

--- a/solution.py
+++ b/solution.py
@@ -33,11 +33,23 @@
 def kernel(
     sizes,
     count_ref,
-    fields_ref,
+    ensemble_ref,
+    diffusion_hbm,
+    drift_rows_hbm,
+    drift_cols_hbm,
+    cells_hbm,
+    values_hbm,
+    weights_hbm,
+    out_ref,
+    raw,
+    diffusion_ref,
+    drift_rows_ref,
+    drift_cols_ref,
     cells_ref,
     values_ref,
     weights_ref,
-    out_ref,
+    top_rows,
+    bottom_rows,
     field_a,
     field_b,
     strip_a,
@@ -65,6 +77,8 @@
     centre_buf,
     result,
     load_sem,
+    small_sem,
+    ready_sem,
     halo_send,
     halo_recv,
     peer_send,
@@ -86,27 +100,78 @@
 
     down, up = other(me_d, 1, n_domain), other(me_d, -1, n_domain)
     right, left = other(me_r, 1, n_role), other(me_r, -1, n_role)
-
-    load = pltpu.make_async_copy(fields_ref, field_a.at[4 : 4 + rows], load_sem.at[0])
+    is_first, is_last = me_d == 0, me_d == n_domain - 1
+
+    load = pltpu.make_async_copy(ensemble_ref, raw, load_sem.at[0])
     load.start()
+    smalls = [
+        pltpu.make_async_copy(src, dst, small_sem.at[k])
+        for k, (src, dst) in enumerate(
+            (
+                (diffusion_hbm, diffusion_ref),
+                (drift_rows_hbm, drift_rows_ref),
+                (drift_cols_hbm, drift_cols_ref),
+                (cells_hbm, cells_ref),
+                (values_hbm, values_ref),
+                (weights_hbm, weights_ref),
+            )
+        )
+    ]
+    for copy in smalls:
+        copy.start()
 
     barrier = pltpu.get_barrier_semaphore()
-    greeted = 0
-    for d in (down, up):
-        for r in (me_r, right, left):
-            pl.semaphore_signal(barrier, inc=1, device_id={"domain": d, "role": r}, device_id_type=MESH)
-            greeted += 1
+    greeted = n_role - 1 + n_member - 1
+    columns = (me_r, right, left)
+
+    def greet(sem, domain):
+        for r in columns:
+            pl.semaphore_signal(sem, inc=1, device_id={"domain": domain, "role": r}, device_id_type=MESH)
+
+    @pl.when(is_first)
+    def _():
+        greet(barrier, up)
+
+    @pl.when(jnp.logical_not(is_last))
+    def _():
+        greet(barrier, down)
+
     for step in range(1, n_role):
         pl.semaphore_signal(barrier, inc=1, device_id={"role": other(me_r, step, n_role)}, device_id_type=MESH)
-        greeted += 1
     for step in range(1, n_member):
         pl.semaphore_signal(barrier, inc=1, device_id={"member": other(me_m, step, n_member)}, device_id_type=MESH)
-        greeted += 1
 
     lane = lax.broadcasted_iota(jnp.int32, (GROUP, LANES), 1)
+    sub = lax.broadcasted_iota(jnp.int32, (GROUP, LANES), 0)
     seg_lane = lane
     for s in range(1, 6):
         seg_lane = jnp.where(lane >= SEG * s, lane - SEG * s, seg_lane)
+
+    for copy in smalls:
+        copy.wait()
+    load.wait()
+
+    def coef_row(row):
+        diffusion = diffusion_ref[pl.ds(row, 1), :]
+        drift_rows = drift_rows_ref[pl.ds(row, 1), :]
+        drift_cols = drift_cols_ref[pl.ds(row, 1), :]
+        keep = 1.0 - 4.0 * diffusion - drift_rows - drift_cols
+        behind_row, behind_col = diffusion + drift_rows, diffusion + drift_cols
+        return jnp.where(
+            sub == 0, keep,
+            jnp.where(sub == 1, diffusion, jnp.where(sub == 2, behind_row, behind_col)),
+        )
+
+    def turn(i, carry):
+        for t in range(8):
+            row = 8 * i + t
+            field_a[row + 4, :members, :] = raw[pl.ds(row, members, stride=rows), :]
+            field_a[row + 4, members:, :] = coef_row(row)
+        return carry
+
+    lax.fori_loop(0, rows // 8, turn, 0)
+    top_rows[...] = field_a[4:8]
+    bottom_rows[...] = field_a[rows : rows + 4]
 
     def own_strip(row):
         strip = jnp.zeros((GROUP, LANES), F32)
@@ -118,8 +183,6 @@
             strip = jnp.where((lane >= base) & (lane < base + 8), ends, strip)
             strip = jnp.where((lane >= base + 16) & (lane < base + 24), starts, strip)
         return strip
-
-    load.wait()
 
     def pack(q, carry):
         to_right = to_left = jnp.zeros((GROUP, LANES), F32)
@@ -136,7 +199,17 @@
         pack_left[q] = to_left
         return carry
 
-    pl.semaphore_wait(barrier, greeted)
+    after_first = (me_d + n_domain - 1) // n_domain
+    at_last = (me_d + 1) // n_domain
+    pl.semaphore_wait(barrier, greeted + 3 * after_first + 3 * at_last)
+
+    @pl.when(jnp.logical_not(is_first))
+    def _():
+        greet(ready_sem.at[0], up)
+
+    @pl.when(is_last)
+    def _():
+        greet(ready_sem.at[1], down)
 
     def halo_copy(k, src, dst, where):
         return pltpu.make_async_remote_copy(
@@ -145,30 +218,100 @@
         )
 
     quads = rows // 4
-    row_halos = [
-        halo_copy(0, fields_ref.at[rows - 4 : rows], field_a.at[0:4], {"domain": down}),
-        halo_copy(1, fields_ref.at[0:4], field_a.at[rows + 4 : rows + 8], {"domain": up}),
-    ]
-    for copy in row_halos:
-        copy.start()
-    lax.fori_loop(0, quads, pack, 0, unroll=2)
-    col_halos = [
-        halo_copy(4, pack_right.at[quads - 1], halo_left.at[0], {"domain": down, "role": right}),
-        halo_copy(5, pack_right.at[0], halo_left.at[quads + 1], {"domain": up, "role": right}),
-        halo_copy(6, pack_left.at[quads - 1], halo_right.at[0], {"domain": down, "role": left}),
-        halo_copy(7, pack_left.at[0], halo_right.at[quads + 1], {"domain": up, "role": left}),
+    rows_down = halo_copy(0, bottom_rows, field_a.at[0:4], {"domain": down})
+    rows_up = halo_copy(1, top_rows, field_a.at[rows + 4 : rows + 8], {"domain": up})
+    sides = [
         halo_copy(2, pack_right, halo_left.at[1 : quads + 1], {"role": right}),
         halo_copy(3, pack_left, halo_right.at[1 : quads + 1], {"role": left}),
     ]
-    for copy in col_halos:
+    corners_down = [
+        halo_copy(4, pack_right.at[quads - 1], halo_left.at[0], {"domain": down, "role": right}),
+        halo_copy(6, pack_left.at[quads - 1], halo_right.at[0], {"domain": down, "role": left}),
+    ]
+    corners_up = [
+        halo_copy(5, pack_right.at[0], halo_left.at[quads + 1], {"domain": up, "role": right}),
+        halo_copy(7, pack_left.at[0], halo_right.at[quads + 1], {"domain": up, "role": left}),
+    ]
+
+    @pl.when(jnp.logical_not(is_first))
+    def _():
+        rows_up.start()
+
+    @pl.when(is_last)
+    def _():
+        rows_down.start()
+
+    lax.fori_loop(0, quads, pack, 0, unroll=2)
+    for copy in sides:
         copy.start()
-    for copy in row_halos:
-        copy.wait()
-    for t in range(4):
-        strip_a[t] = own_strip(t)
-        strip_a[rows + 4 + t] = own_strip(rows + 4 + t)
-    for copy in col_halos:
-        copy.wait()
+
+    @pl.when(jnp.logical_not(is_first))
+    def _():
+        for copy in corners_up:
+            copy.start()
+
+    @pl.when(jnp.logical_not(is_last))
+    def _():
+        pl.semaphore_wait(ready_sem.at[0], 3)
+        rows_down.start()
+
+    for copy in corners_down:
+        copy.start()
+
+    def advanced(now, before, after, coef):
+        axis = now.ndim - 1
+        return (
+            now * coef[0]
+            + (after + pltpu.roll(now, LANES - 1, axis)) * coef[1]
+            + before * coef[2]
+            + pltpu.roll(now, 1, axis) * coef[3]
+        )
+
+    def field_coef(row):
+        return [field_a[row, members + k : members + k + 1, :] for k in range(4)]
+
+    def field_rows(source, target, shift, first, amount):
+        before = source[first - 1, :members, :]
+        now = source[first, :members, :]
+        for i in range(amount):
+            row = first + i
+            after = source[row + 1, :members, :]
+            target[row - shift, :members, :] = advanced(now, before, after, field_coef(row))
+            before, now = now, after
+
+    def seam_rows(source, first, amount):
+        span, back, ahead = (slice(first + k, first + k + amount) for k in (0, -1, 1))
+        coef = [strip_coef[span, k : k + 1, :] for k in range(4)]
+        return advanced(source[span], source[back], source[ahead], coef)
+
+    def merge(seam, first, amount):
+        for i in range(amount):
+            for s in range(groups):
+                part = slice(GROUP * s, GROUP * (s + 1))
+                begin = pltpu.roll(seam[i], (-(SEG * s + 16)) % LANES, 1)
+                end = pltpu.roll(seam[i], (120 - SEG * s) % LANES, 1)
+                block = final[first - 4 + i, part, :]
+                final[first - 4 + i, part, :] = jnp.where(
+                    lane < 4, begin, jnp.where(lane >= LANES - 4, end, block)
+                )
+
+    fields = (field_a, field_b, field_a, field_b, final)
+    strips = (strip_a, strip_b, strip_a, strip_b)
+    for step in range(STEPS):
+        first, end = 5 + step, rows + 3 - step
+        shift = 4 if step == STEPS - 1 else 0
+        whole = (end - first) // 10
+
+        def body(i, carry, step=step, first=first, shift=shift):
+            field_rows(fields[step], fields[step + 1], shift, first + 10 * i, 10)
+            return carry
+
+        lax.fori_loop(0, whole, body, 0)
+        if end - first - 10 * whole:
+            field_rows(fields[step], fields[step + 1], shift, first + 10 * whole, end - first - 10 * whole)
+
+    for copy in sides:
+        copy.wait_recv()
 
     def unpack(q, carry):
         from_left = halo_left[q]
@@ -188,73 +331,37 @@
             strip_coef[row] = coef
         return carry
 
-    lax.fori_loop(0, quads + 2, unpack, 0, unroll=2)
-
-    def advanced(now, before, after, coef):
-        return (
-            now * coef[0]
-            + (after + pltpu.roll(now, LANES - 1, 1)) * coef[1]
-            + before * coef[2]
-            + pltpu.roll(now, 1, 1) * coef[3]
-        )
-
-    def field_coef(row):
-        return [field_a[row, members + k : members + k + 1, :] for k in range(4)]
-
-    def seam_coef(row):
-        return [strip_coef[row, k : k + 1, :] for k in range(4)]
-
-    def step_rows(source, target, strip_source, strip_target, first, amount):
-        before = source[first - 1, :members, :]
-        now = source[first, :members, :]
-        seam_before = strip_source[first - 1]
-        seam_now = strip_source[first]
-        for i in range(amount):
-            row = first + i
-            after = source[row + 1, :members, :]
-            seam_after = strip_source[row + 1]
-            target[row, :members, :] = advanced(now, before, after, field_coef(row))
-            strip_target[row] = advanced(seam_now, seam_before, seam_after, seam_coef(row))
-            before, now = now, after
-            seam_before, seam_now = seam_now, seam_after
-
-    pairs = ((field_a, field_b, strip_a, strip_b), (field_b, field_a, strip_b, strip_a))
-    for step in range(STEPS - 1):
-
-        def body(i, carry, refs=pairs[step % 2]):
-            step_rows(*refs, 1 + 10 * i, 10)
-            return carry
-
-        lax.fori_loop(0, 7, body, 0)
-
-    source, _, strip_source, _ = pairs[(STEPS - 1) % 2]
-
-    def last_rows(first, amount):
-        before = source[first - 1, :members, :]
-        now = source[first, :members, :]
-        seam_before = strip_source[first - 1]
-        seam_now = strip_source[first]
-        for i in range(amount):
-            row = first + i
-            after = source[row + 1, :members, :]
-            seam_after = strip_source[row + 1]
-            new = advanced(now, before, after, field_coef(row))
-            seam = advanced(seam_now, seam_before, seam_after, seam_coef(row))
-            for s in range(groups):
-                begin = pltpu.roll(seam, (-(SEG * s + 16)) % LANES, 1)
-                end = pltpu.roll(seam, (120 - SEG * s) % LANES, 1)
-                block = new[GROUP * s : GROUP * (s + 1), :]
-                block = jnp.where(lane < 4, begin, jnp.where(lane >= LANES - 4, end, block))
-                final[row - 4, GROUP * s : GROUP * (s + 1), :] = block
-            before, now = now, after
-            seam_before, seam_now = seam_now, seam_after
-
-    def last_body(i, carry):
-        last_rows(4 + 8 * i, 8)
-        return carry
-
-    lax.fori_loop(0, rows // 8, last_body, 0)
-
+    lax.fori_loop(1, quads + 1, unpack, 0, unroll=2)
+
+    for step in range(STEPS):
+        first, end = 5 + step, rows + 3 - step
+        while first < end:
+            amount = min(16 if step < STEPS - 1 else 8, end - first)
+            seam = seam_rows(strips[step], first, amount)
+            if step < STEPS - 1:
+                strips[step + 1][first : first + amount] = seam
+            else:
+                merge(seam, first, amount)
+            first += amount
+
+    def edge(first, last):
+        for step in range(STEPS):
+            shift = 4 if step == STEPS - 1 else 0
+            begin = first + step if last else first - step
+            field_rows(fields[step], fields[step + 1], shift, begin, 4)
+            seam = seam_rows(strips[step], begin, 4)
+            if step < STEPS - 1:
+                strips[step + 1][begin : begin + 4] = seam
+            else:
+                merge(seam, begin, 4)
+
+    rows_up.wait_recv()
+    for copy in corners_up:
+        copy.wait_recv()
+    for t in range(4):
+        strip_a[rows + 4 + t] = own_strip(rows + 4 + t)
+    unpack(quads + 1, 0)
+    edge(rows + 3, False)
     def peer_copy(stage, step, src, dst, axis):
         me, n = (me_m, n_member) if axis == "member" else (me_r, n_role)
         return pltpu.make_async_remote_copy(
@@ -263,42 +370,69 @@
         )
 
     order = sorted(range(1, n_member), key=lambda s: -min(s, n_member - s))
-    forward = []
+    mine = pl.ds(pl.multiple_of(members * me_m, members), members)
+    forward = {}
     for step in order:
         first = pl.multiple_of(chunk * other(me_m, step, n_member), chunk)
-        forward.append(
-            peer_copy(
-                0, step, final.at[pl.ds(first, chunk)],
-                received.at[:, pl.ds(pl.multiple_of(members * me_m, members), members), :], "member",
-            )
-        )
+        forward[step] = peer_copy(0, step, final.at[pl.ds(first, chunk)], received.at[:, mine, :], "member")
     keep = pltpu.make_async_copy(
-        final.at[pl.ds(pl.multiple_of(chunk * me_m, chunk), chunk)],
-        received.at[:, pl.ds(pl.multiple_of(members * me_m, members), members), :],
-        load_sem.at[1],
+        final.at[pl.ds(pl.multiple_of(chunk * me_m, chunk), chunk)], received.at[:, mine, :], load_sem.at[1]
     )
-    early = 2
-    for copy in forward[:early]:
-        copy.start()
-
-    def observe(g, carry):
-        cell = cells_ref[pl.ds(g, 1), :]
-        here = ((cell // LANES) % n_role) == me_r
-        row_of = jnp.where(here, cell // (LANES * n_role), -1)
-        row_of = jnp.broadcast_to(row_of, (members, LANES))
-        col_of = jnp.broadcast_to(cell % LANES, (members, LANES))
-
-        def some(q, seen):
-            for t in range(16):
-                row = 16 * q + t
-                picked = jnp.take_along_axis(final[row], col_of, axis=1, mode="promise_in_bounds")
-                seen = jnp.where(row_of == row, picked, seen)
-            return seen
-
-        obs_part[g] = lax.fori_loop(0, rows // 16, some, jnp.zeros((members, LANES), F32))
-        return carry
-
-    lax.fori_loop(0, 8, observe, 0)
+    early = [s for s in order[::-1] if min(s, n_member - s) <= 2]
+    late = [s for s in order if s not in early]
+
+    def start_early(inner):
+        for step in early:
+            whom = other(me_m, step, n_member)
+            ready = whom > 0
+
+            @pl.when(ready if inner else jnp.logical_not(ready))
+            def _(copy=forward[step]):
+                copy.start()
+
+    start_early(True)
+
+    def observe(begin, part, parts):
+        def of_group(g, carry):
+            cell = cells_ref[pl.ds(g, 1), :]
+            here = ((cell // LANES) % n_role) == me_r
+            row_of = jnp.where(here, cell // (LANES * n_role), -1)
+            row_of = jnp.broadcast_to(row_of, (members, LANES))
+            col_of = jnp.broadcast_to(cell % LANES, (members, LANES))
+
+            def some(q, seen):
+                for t in range(part):
+                    row = begin + part * q + t
+                    picked = jnp.take_along_axis(final[row], col_of, axis=1, mode="promise_in_bounds")
+                    seen = jnp.where(row_of == row, picked, seen)
+                return seen
+
+            if parts > 1:
+                obs_part[g] = lax.fori_loop(0, parts, some, jnp.zeros((members, LANES), F32))
+            else:
+                obs_part[g] = some(0, obs_part[g])
+            return carry
+
+        lax.fori_loop(0, 8, of_group, 0)
+
+    observe(4, 15, 4)
+
+    @pl.when(is_first)
+    def _():
+        pl.semaphore_wait(ready_sem.at[1], 3)
+        rows_up.start()
+        for copy in corners_up:
+            copy.start()
+
+    rows_down.wait_recv()
+    for copy in corners_down:
+        copy.wait_recv()
+    for t in range(4):
+        strip_a[t] = own_strip(t)
+    unpack(0, 0)
+    edge(1, True)
+    start_early(False)
+    observe(0, 4, 1)
 
     def own_groups(r):
         return pl.ds(slot_groups * r, slot_groups)
@@ -314,17 +448,16 @@
         copy.wait()
     obs_own[...] = functools.reduce(jnp.add, [obs_role[r] for r in range(n_role)])
 
-    mine = pl.ds(pl.multiple_of(members * me_m, members), members)
     copies = []
     for step in order:
         copies.append(peer_copy(2, step, obs_own, obs_all.at[:, mine, :], "member"))
         copies[-1].start()
-    for copy in forward[early:]:
-        copy.start()
     keep.start()
     obs_all[:, mine, :] = obs_own[...]
     for copy in copies:
         copy.wait()
+    for step in late:
+        forward[step].start()
 
     part = jnp.zeros((total, total), F32)
     push = jnp.zeros((GROUP, total), F32)
@@ -391,8 +524,8 @@
     shifted = product(halves(product(halves(innovation), root_halves)), root_halves) / scaling
     mixing[...] = root * jnp.sqrt((total - 1.0) / scaling) + shifted[0:1, :]
 
-    for copy in forward:
-        copy.wait()
+    for step in order:
+        forward[step].wait()
     keep.wait()
     for i in range(chunk):
         block = received[i]
@@ -417,25 +550,19 @@
             copy = pltpu.make_async_copy(result.at[step], out_ref.at[target_rows], load_sem.at[2])
         copy.start()
         back.append(copy)
-    for copy in back:
-        copy.wait()
+    for copy in back[:-1]:
+        copy.wait_send()
+    for step in order[::-1]:
+        back[order.index(step)].wait_recv()
+    back[-1].wait()
+    for copy in [rows_down, rows_up] + sides + corners_down + corners_up:
+        copy.wait_send()
 
 
 def shards(sizes, ensemble, diffusion, drift_rows, drift_cols, cells, count, values, weights):
     n_member, n_domain, n_role = sizes
     members, rows, cols = ensemble.shape
     total = members * n_member
-    coef = jnp.stack(
-        [
-            1.0 - 4.0 * diffusion - drift_rows - drift_cols,
-            diffusion,
-            diffusion + drift_rows,
-            diffusion + drift_cols,
-        ]
-        + [jnp.zeros_like(diffusion)] * 4,
-        axis=1,
-    )
-    fields = jnp.concatenate([jnp.transpose(ensemble, (1, 0, 2)), coef], axis=1)
     planes = members + GROUP
     chunk = rows // n_member
     slot_groups = 8 // n_role
@@ -450,15 +577,18 @@
         functools.partial(kernel, (n_member, n_domain, n_role, members)),
         name="forecast_analysis",
         out_shape=jax.ShapeDtypeStruct((rows, members, cols), F32),
-        in_specs=[
-            pl.BlockSpec(memory_space=pltpu.SMEM),
-            pl.BlockSpec(memory_space=pl.ANY),
-            pl.BlockSpec(memory_space=pltpu.VMEM),
-            pl.BlockSpec(memory_space=pltpu.VMEM),
-            pl.BlockSpec(memory_space=pltpu.VMEM),
-        ],
+        in_specs=[pl.BlockSpec(memory_space=pltpu.SMEM)] + [pl.BlockSpec(memory_space=pltpu.HBM)] * 7,
         out_specs=pl.BlockSpec(memory_space=pl.ANY),
         scratch_shapes=[
+            vmem(members * rows, cols),
+            vmem(rows, cols),
+            vmem(rows, cols),
+            vmem(rows, cols),
+            vmem(8, LANES, dtype=jnp.int32),
+            vmem(8, LANES),
+            vmem(8, LANES),
+            vmem(4, planes, cols),
+            vmem(4, planes, cols),
             vmem(rows + 8, planes, cols),
             vmem(rows + 8, planes, cols),
             vmem(rows + 8, GROUP, LANES),
@@ -486,6 +616,8 @@
             vmem(1, chunk * cols),
             vmem(n_member, chunk, members, cols),
             pltpu.SemaphoreType.DMA((3,)),
+            pltpu.SemaphoreType.DMA((6,)),
+            pltpu.SemaphoreType.REGULAR((2,)),
             pltpu.SemaphoreType.DMA((8,)),
             pltpu.SemaphoreType.DMA((8,)),
             pltpu.SemaphoreType.DMA((6, 8)),
@@ -496,10 +628,18 @@
         ),
     )(
         count,
-        fields,
-        cells.reshape(8, LANES),
-        values.reshape(8, LANES),
-        weights.reshape(8, LANES),
+        *(
+            pltpu.with_memory_space_constraint(a, pltpu.HBM)
+            for a in (
+                ensemble.reshape(members * rows, cols),
+                diffusion,
+                drift_rows,
+                drift_cols,
+                cells.reshape(8, LANES),
+                values.reshape(8, LANES),
+                weights.reshape(8, LANES),
+            )
+        ),
     )
     return jnp.transpose(out, (1, 0, 2))
 

time: 98.8 us -> 81.2 us (0.82)
  Pallas kernels: 93 us -> 78.8 us
  local copies, waits for them, and re-layouts: 3.93 us -> 1.58 us
    pallas_call x1, Pallas kernels: 93 us -> 78.8 us  [shards(): pl.pallas_call(functools.partial(kernel, (n_member, n_domain, n_role, mem...]
    unnamed x9 -> x0, local copies, waits for them, and re-layouts: 1.86 us -> none
where the time goes in v2:
time: 81.2 us; the launch traced here: 81.1 us
  Pallas kernels  78.8 us (97%)
  local copies, waits for them, and re-layouts  1.58 us (2%)
    pallas_call x1, Pallas kernels, shards(): pl.pallas_call(functools.partial(kernel, (n_member, n_domain, n_role, mem...  78.8 us

profile of v2, /device:TPU:1, one launch (start us, length us, event | category | flops | bytes accessed | tf_op | source)
XLA Modules:
  0.0 81.1 jit_solution(16285870540665852742)
XLA Ops:
  0.7 78.8 %forecast_analysis.1 = f32[64,32,128]{2,1,0:T(8,128)S(1)} custom-call(s32[1]{0:T(128)S(6)} %copy.10.count_ref, f32[2048,128]{1,0:T(8,128)} %bitcast.6, f32[64,128]{1,0:T(8,128)} %diffusion_hbm.1, f32[64,128]{1,0:T(8,128)} %drift_rows_hbm.1, f32[64,128]{1,0:T(8,128)} %drift_cols_hbm.1, s32[8,128]{1,0:T(8,128)} %bitcast.7, f32[8,128]{1,0:T(8,128)} %bitcast.8, ...), custom_call_target="tpu_custom_call" | custom-call | tf_op jit(solution)/shard_map/forecast_analysis/pallas_call | solution.py:576
  79.5 1.6 %copy.9 = f32[32,64,128]{2,1,0:T(8,128)} copy(f32[32,64,128]{2,0,1:T(8,128)S(1)} %bitcast.5) | data formatting | bytes 2097152 | tf_op jit(solution)/shard_map/transpose | solution.py:644

commit v3 on v2

--- a/solution.py
+++ b/solution.py
@@ -67,6 +67,8 @@
     obs_all,
     gram_part,
     gram_role,
+    push_own,
+    push_role,
     gram_own,
     gram,
     current,
@@ -241,21 +243,21 @@
     def _():
         rows_down.start()
 
-    lax.fori_loop(0, quads, pack, 0, unroll=2)
-    for copy in sides:
-        copy.start()
+    pack(quads - 1, 0)
+    pack(0, 0)
+
+    @pl.when(is_last)
+    def _():
+        for copy in corners_down:
+            copy.start()
 
     @pl.when(jnp.logical_not(is_first))
     def _():
         for copy in corners_up:
             copy.start()
 
-    @pl.when(jnp.logical_not(is_last))
-    def _():
-        pl.semaphore_wait(ready_sem.at[0], 3)
-        rows_down.start()
-
-    for copy in corners_down:
+    lax.fori_loop(1, quads - 1, pack, 0, unroll=2)
+    for copy in sides:
         copy.start()
 
     def advanced(now, before, after, coef):
@@ -300,15 +302,20 @@
     for step in range(STEPS):
         first, end = 5 + step, rows + 3 - step
         shift = 4 if step == STEPS - 1 else 0
-        whole = (end - first) // 10
-
-        def body(i, carry, step=step, first=first, shift=shift):
-            field_rows(fields[step], fields[step + 1], shift, first + 10 * i, 10)
+        half = (end - first) // 2
+
+        def body(i, carry, step=step, first=first, shift=shift, half=half):
+            field_rows(fields[step], fields[step + 1], shift, first + half * i, half)
             return carry
 
-        lax.fori_loop(0, whole, body, 0)
-        if end - first - 10 * whole:
-            field_rows(fields[step], fields[step + 1], shift, first + 10 * whole, end - first - 10 * whole)
+        lax.fori_loop(0, 2, body, 0)
+
+    @pl.when(jnp.logical_not(is_last))
+    def _():
+        pl.semaphore_wait(ready_sem.at[0], 3)
+        rows_down.start()
+        for copy in corners_down:
+            copy.start()
 
     for copy in sides:
         copy.wait_recv()
@@ -331,12 +338,12 @@
             strip_coef[row] = coef
         return carry
 
-    lax.fori_loop(1, quads + 1, unpack, 0, unroll=2)
+    lax.fori_loop(1, quads + 1, unpack, 0, unroll=4)
 
     for step in range(STEPS):
         first, end = 5 + step, rows + 3 - step
         while first < end:
-            amount = min(16 if step < STEPS - 1 else 8, end - first)
+            amount = min(31 if step < STEPS - 1 else 14, end - first)
             seam = seam_rows(strips[step], first, amount)
             if step < STEPS - 1:
                 strips[step + 1][first : first + amount] = seam
@@ -392,30 +399,22 @@
 
     start_early(True)
 
-    def observe(begin, part, parts):
-        def of_group(g, carry):
-            cell = cells_ref[pl.ds(g, 1), :]
-            here = ((cell // LANES) % n_role) == me_r
-            row_of = jnp.where(here, cell // (LANES * n_role), -1)
-            row_of = jnp.broadcast_to(row_of, (members, LANES))
-            col_of = jnp.broadcast_to(cell % LANES, (members, LANES))
-
-            def some(q, seen):
-                for t in range(part):
-                    row = begin + part * q + t
-                    picked = jnp.take_along_axis(final[row], col_of, axis=1, mode="promise_in_bounds")
-                    seen = jnp.where(row_of == row, picked, seen)
-                return seen
-
-            if parts > 1:
-                obs_part[g] = lax.fori_loop(0, parts, some, jnp.zeros((members, LANES), F32))
-            else:
-                obs_part[g] = some(0, obs_part[g])
-            return carry
-
-        lax.fori_loop(0, 8, of_group, 0)
-
-    observe(4, 15, 4)
+    def observe(g, begin, end, seen):
+        cell = cells_ref[pl.ds(g, 1), :]
+        here = ((cell // LANES) % n_role) == me_r
+        row_of = jnp.where(here, cell // (LANES * n_role), -1)
+        row_of = jnp.broadcast_to(row_of, (members, LANES))
+        col_of = jnp.broadcast_to(cell % LANES, (members, LANES))
+        for row in range(begin, end):
+            picked = jnp.take_along_axis(final[row], col_of, axis=1, mode="promise_in_bounds")
+            seen = jnp.where(row_of == row, picked, seen)
+        obs_part[g] = seen
+
+    def observe_group(g, carry):
+        observe(g, 4, rows, jnp.zeros((members, LANES), F32))
+        return carry
+
+    lax.fori_loop(0, 8, observe_group, 0)
 
     @pl.when(is_first)
     def _():
@@ -432,17 +431,19 @@
     unpack(0, 0)
     edge(1, True)
     start_early(False)
-    observe(0, 4, 1)
 
     def own_groups(r):
         return pl.ds(slot_groups * r, slot_groups)
 
     copies = []
-    for step in range(1, n_role):
-        copies.append(
-            peer_copy(1, step, obs_part.at[own_groups(other(me_r, step, n_role))], obs_role.at[me_r], "role")
-        )
-        copies[-1].start()
+    for step in list(range(1, n_role)) + [0]:
+        whom = other(me_r, step, n_role)
+        for k in range(slot_groups):
+            g = slot_groups * whom + k
+            observe(g, 0, 4, obs_part[g])
+        if step:
+            copies.append(peer_copy(1, step, obs_part.at[own_groups(whom)], obs_role.at[me_r], "role"))
+            copies[-1].start()
     obs_role[me_r] = obs_part[own_groups(me_r)]
     for copy in copies:
         copy.wait()
@@ -474,8 +475,8 @@
         part = part + product(halves(deviation), weighted, NT)
         push = push + product(halves(gap), weighted, NT)
     for r in range(n_role):
-        gram_part[r, :gram_rows, :] = part[gram_rows * r : gram_rows * (r + 1), :]
-        gram_part[r, gram_rows:, :] = push
+        gram_part[r] = part[gram_rows * r : gram_rows * (r + 1), :]
+    push_own[...] = push[0:1, :]
 
     copies = []
     for step in range(1, n_role):
@@ -483,12 +484,15 @@
             peer_copy(3, step, gram_part.at[other(me_r, step, n_role)], gram_role.at[me_r], "role")
         )
         copies[-1].start()
+    pushes = []
+    for step in range(1, n_role):
+        pushes.append(peer_copy(6, step, push_own, push_role.at[me_r], "role"))
+        pushes[-1].start()
     gram_role[me_r] = gram_part[me_r]
+    push_role[me_r] = push_own[...]
     for copy in copies:
         copy.wait()
-    summed = functools.reduce(jnp.add, [gram_role[r] for r in range(n_role)])
-    innovation = summed[gram_rows:, :]
-    gram_own[...] = summed[:gram_rows, :]
+    gram_own[...] = functools.reduce(jnp.add, [gram_role[r] for r in range(n_role)])
     band = pl.ds(pl.multiple_of(gram_rows * me_r, gram_rows), gram_rows)
     copies = []
     for step in range(1, n_role):
@@ -517,6 +521,10 @@
         return carry
 
     lax.fori_loop(0, ITERS - 2, newton, 0)
+    for copy in pushes:
+        copy.wait()
+    innovation = functools.reduce(jnp.add, [push_role[r] for r in range(n_role)])
+    innovation = jnp.broadcast_to(innovation, (GROUP, total))
     inv = halves(inverse[...])
     mid = halves(jnp.where(diagonal, 1.5, 0.0) - 0.5 * product(inv, halves(current[...])))
     root = product(mid, inv)
@@ -604,8 +612,10 @@
             vmem(n_role, slot_groups, members, LANES),
             vmem(slot_groups, members, LANES),
             vmem(slot_groups, total, LANES),
-            vmem(n_role, gram_rows + GROUP, total),
-            vmem(n_role, gram_rows + GROUP, total),
+            vmem(n_role, gram_rows, total),
+            vmem(n_role, gram_rows, total),
+            vmem(1, total),
+            vmem(n_role, 1, total),
             vmem(gram_rows, total),
             vmem(total, total),
             vmem(total, total),
@@ -620,8 +630,8 @@
             pltpu.SemaphoreType.REGULAR((2,)),
             pltpu.SemaphoreType.DMA((8,)),
             pltpu.SemaphoreType.DMA((8,)),
-            pltpu.SemaphoreType.DMA((6, 8)),
-            pltpu.SemaphoreType.DMA((6, 8)),
+            pltpu.SemaphoreType.DMA((7, 8)),
+            pltpu.SemaphoreType.DMA((7, 8)),
         ],
         compiler_params=pltpu.CompilerParams(
             collective_id=0, has_side_effects=True, vmem_limit_bytes=40 << 20

time: 81.2 us -> 80.1 us (0.986)
  Pallas kernels: 78.8 us -> 77.7 us
    pallas_call x1, Pallas kernels: 78.8 us -> 77.7 us  [shards(): pl.pallas_call(functools.partial(kernel, (n_member, n_domain, n_role, mem...]
where the time goes in v3:
time: 80.1 us; the launch traced here: 79.9 us
  Pallas kernels  77.7 us (97%)
  local copies, waits for them, and re-layouts  1.58 us (2%)
    pallas_call x1, Pallas kernels, shards(): pl.pallas_call(functools.partial(kernel, (n_member, n_domain, n_role, mem...  77.7 us

profile of v3, /device:TPU:1, one launch (start us, length us, event | category | flops | bytes accessed | tf_op | source)
XLA Modules:
  0.0 79.9 jit_solution(7172315173092427050)
XLA Ops:
  0.7 77.7 %forecast_analysis.1 = f32[64,32,128]{2,1,0:T(8,128)S(1)} custom-call(s32[1]{0:T(128)S(6)} %copy.10.count_ref, f32[2048,128]{1,0:T(8,128)} %bitcast.6, f32[64,128]{1,0:T(8,128)} %diffusion_hbm.1, f32[64,128]{1,0:T(8,128)} %drift_rows_hbm.1, f32[64,128]{1,0:T(8,128)} %drift_cols_hbm.1, s32[8,128]{1,0:T(8,128)} %bitcast.7, f32[8,128]{1,0:T(8,128)} %bitcast.8, ...), custom_call_target="tpu_custom_call" | custom-call | tf_op jit(solution)/shard_map/forecast_analysis/pallas_call | solution.py:584
  78.3 1.6 %copy.9 = f32[32,64,128]{2,1,0:T(8,128)} copy(f32[32,64,128]{2,0,1:T(8,128)S(1)} %bitcast.5) | data formatting | bytes 2097152 | tf_op jit(solution)/shard_map/transpose | solution.py:654

commit v4 on v3

--- a/solution.py
+++ b/solution.py
@@ -79,6 +79,7 @@
     centre_buf,
     result,
     load_sem,
+    whole_sem,
     small_sem,
     ready_sem,
     halo_send,
@@ -104,8 +105,15 @@
     right, left = other(me_r, 1, n_role), other(me_r, -1, n_role)
     is_first, is_last = me_d == 0, me_d == n_domain - 1
 
-    load = pltpu.make_async_copy(ensemble_ref, raw, load_sem.at[0])
-    load.start()
+    quarter = members * rows // 4
+    loads = [
+        pltpu.make_async_copy(
+            ensemble_ref.at[k * quarter : (k + 1) * quarter], raw.at[k * quarter : (k + 1) * quarter], whole_sem.at[k]
+        )
+        for k in range(4)
+    ]
+    for copy in loads:
+        copy.start()
     smalls = [
         pltpu.make_async_copy(src, dst, small_sem.at[k])
         for k, (src, dst) in enumerate(
@@ -149,9 +157,8 @@
     for s in range(1, 6):
         seg_lane = jnp.where(lane >= SEG * s, lane - SEG * s, seg_lane)
 
-    for copy in smalls:
+    for copy in smalls + loads:
         copy.wait()
-    load.wait()
 
     def coef_row(row):
         diffusion = diffusion_ref[pl.ds(row, 1), :]
@@ -175,30 +182,38 @@
     top_rows[...] = field_a[4:8]
     bottom_rows[...] = field_a[rows : rows + 4]
 
+    def stacked(pieces, masks):
+        whole = pieces[0]
+        for piece, mask in zip(pieces[1:], masks):
+            whole = jnp.where(mask, piece, whole)
+        return whole
+
+    def turned(value, shift):
+        return pltpu.roll(value, shift % LANES, value.ndim - 1) if shift % LANES else value
+
+    strip_masks = [lane >= SEG * (k // 2) + 16 * (k % 2) for k in range(1, 2 * groups + 2)]
+    quad_masks = [seg_lane >= 8, seg_lane >= 12, seg_lane >= 16]
+    halo_mask = quad_masks[0] & (seg_lane < 16)
+    seg_masks = [lane >= SEG * s for s in range(1, groups)]
+
     def own_strip(row):
-        strip = jnp.zeros((GROUP, LANES), F32)
+        pieces = []
         for s in range(groups + 1):
             block = field_a[row, GROUP * s : GROUP * (s + 1), :]
-            base = SEG * s
-            ends = pltpu.roll(block, (base + 8) % LANES, 1)
-            starts = pltpu.roll(block, (base + 16) % LANES, 1)
-            strip = jnp.where((lane >= base) & (lane < base + 8), ends, strip)
-            strip = jnp.where((lane >= base + 16) & (lane < base + 24), starts, strip)
-        return strip
-
-    def pack(q, carry):
-        to_right = to_left = jnp.zeros((GROUP, LANES), F32)
-        for t in range(4):
-            row = 4 + 4 * q + t
-            strip = own_strip(row)
-            strip_a[row] = strip
-            low, high = 4 + 4 * t, 16 - 4 * t
-            moved = pltpu.roll(strip, 4 * t, 1) if t else strip
-            to_right = jnp.where((seg_lane >= low) & (seg_lane < low + 4), moved, to_right)
-            moved = pltpu.roll(strip, LANES - 4 * t, 1) if t else strip
-            to_left = jnp.where((seg_lane >= high) & (seg_lane < high + 4), moved, to_left)
-        pack_right[q] = to_right
-        pack_left[q] = to_left
+            pieces += [turned(block, SEG * s + 8), turned(block, SEG * s + 16)]
+        return stacked(pieces, strip_masks)
+
+    def pack(q):
+        own = [strip_a[4 + 4 * q + t] for t in range(4)]
+        pack_right[q] = stacked([turned(own[t], 4 * t) for t in range(4)], quad_masks)
+        pack_left[q] = stacked([turned(own[t], -4 * t) for t in range(3, -1, -1)], quad_masks)
+
+    def own_strips(first, amount):
+        for t in range(amount):
+            strip_a[first + t] = own_strip(first + t)
+
+    def own_block(i, carry):
+        own_strips(8 + 14 * i, 14)
         return carry
 
     after_first = (me_d + n_domain - 1) // n_domain
@@ -243,8 +258,10 @@
     def _():
         rows_down.start()
 
-    pack(quads - 1, 0)
-    pack(0, 0)
+    own_strips(4, 4)
+    own_strips(rows, 4)
+    pack(quads - 1)
+    pack(0)
 
     @pl.when(is_last)
     def _():
@@ -256,7 +273,9 @@
         for copy in corners_up:
             copy.start()
 
-    lax.fori_loop(1, quads - 1, pack, 0, unroll=2)
+    lax.fori_loop(0, 4, own_block, 0)
+    for q in range(1, quads - 1):
+        pack(q)
     for copy in sides:
         copy.start()
 
@@ -302,13 +321,7 @@
     for step in range(STEPS):
         first, end = 5 + step, rows + 3 - step
         shift = 4 if step == STEPS - 1 else 0
-        half = (end - first) // 2
-
-        def body(i, carry, step=step, first=first, shift=shift, half=half):
-            field_rows(fields[step], fields[step + 1], shift, first + half * i, half)
-            return carry
-
-        lax.fori_loop(0, 2, body, 0)
+        field_rows(fields[step], fields[step + 1], shift, first, end - first)
 
     @pl.when(jnp.logical_not(is_last))
     def _():
@@ -325,17 +338,10 @@
         from_right = halo_right[q]
         for t in range(4):
             row = 4 * q + t
-            strip = strip_a[row]
-            moved = pltpu.roll(from_left, (8 - 4 * t) % LANES, 1) if t != 2 else from_left
-            strip = jnp.where((seg_lane >= 12) & (seg_lane < 16), moved, strip)
-            moved = pltpu.roll(from_right, (4 * t - 8) % LANES, 1) if t != 2 else from_right
-            strip = jnp.where((seg_lane >= 8) & (seg_lane < 12), moved, strip)
+            halo = jnp.where(quad_masks[1], turned(from_left, 8 - 4 * t), turned(from_right, 4 * t - 8))
+            strip = jnp.where(halo_mask, halo, strip_a[row])
             strip_a[row] = strip
-            coef = strip
-            for s in range(groups):
-                moved = pltpu.roll(strip, (SEG * (s - groups)) % LANES, 1)
-                coef = jnp.where((lane >= SEG * s) & (lane < SEG * (s + 1)), moved, coef)
-            strip_coef[row] = coef
+            strip_coef[row] = stacked([turned(strip, SEG * (s - groups)) for s in range(groups)], seg_masks)
         return carry
 
     lax.fori_loop(1, quads + 1, unpack, 0, unroll=4)
@@ -411,10 +417,11 @@
         obs_part[g] = seen
 
     def observe_group(g, carry):
-        observe(g, 4, rows, jnp.zeros((members, LANES), F32))
+        for k in range(2):
+            observe(2 * g + k, 4, rows, jnp.zeros((members, LANES), F32))
         return carry
 
-    lax.fori_loop(0, 8, observe_group, 0)
+    lax.fori_loop(0, 4, observe_group, 0)
 
     @pl.when(is_first)
     def _():
@@ -626,6 +633,7 @@
             vmem(1, chunk * cols),
             vmem(n_member, chunk, members, cols),
             pltpu.SemaphoreType.DMA((3,)),
+            pltpu.SemaphoreType.DMA((4,)),
             pltpu.SemaphoreType.DMA((6,)),
             pltpu.SemaphoreType.REGULAR((2,)),
             pltpu.SemaphoreType.DMA((8,)),

time: 80.1 us -> 79.6 us (level)
  no operation moved by 1% of the time
where the time goes in v4:
time: 79.6 us; the launch traced here: 79.4 us
  Pallas kernels  77.2 us (97%)
  local copies, waits for them, and re-layouts  1.58 us (2%)
    pallas_call x1, Pallas kernels, shards(): pl.pallas_call(functools.partial(kernel, (n_member, n_domain, n_role, mem...  77.2 us

profile of v4, /device:TPU:1, one launch (start us, length us, event | category | flops | bytes accessed | tf_op | source)
XLA Modules:
  0.0 79.4 jit_solution(12119969216556290858)
XLA Ops:
  0.7 77.2 %forecast_analysis.1 = f32[64,32,128]{2,1,0:T(8,128)S(1)} custom-call(s32[1]{0:T(128)S(6)} %copy.10.count_ref, f32[2048,128]{1,0:T(8,128)} %bitcast.6, f32[64,128]{1,0:T(8,128)} %diffusion_hbm.1, f32[64,128]{1,0:T(8,128)} %drift_rows_hbm.1, f32[64,128]{1,0:T(8,128)} %drift_cols_hbm.1, s32[8,128]{1,0:T(8,128)} %bitcast.7, f32[8,128]{1,0:T(8,128)} %bitcast.8, ...), custom_call_target="tpu_custom_call" | custom-call | tf_op jit(solution)/shard_map/forecast_analysis/pallas_call | solution.py:591
  77.8 1.6 %copy.9 = f32[32,64,128]{2,1,0:T(8,128)} copy(f32[32,64,128]{2,0,1:T(8,128)S(1)} %bitcast.5) | data formatting | bytes 2097152 | tf_op jit(solution)/shard_map/transpose | solution.py:662

commit v5 on v4

--- a/solution.py
+++ b/solution.py
@@ -71,8 +71,7 @@
     push_role,
     gram_own,
     gram,
-    current,
-    inverse,
+    iterates,
     mixing,
     dev_high,
     dev_low,
@@ -517,14 +516,14 @@
     scaling = jnp.sqrt(squares)
     scaled = matrix / scaling
     middle = jnp.where(diagonal, 1.5, 0.0) - 0.5 * scaled
-    current[...] = product(halves(scaled), halves(middle))
-    inverse[...] = middle
+    iterates[:total] = product(halves(scaled), halves(middle))
+    iterates[total:] = middle
 
     def newton(i, carry):
-        cur, inv = halves(current[...]), halves(inverse[...])
+        high, low = halves(iterates[...])
+        inv, cur = (high[total:], low[total:]), (high[:total], low[:total])
         mid = halves(jnp.where(diagonal, 1.5, 0.0) - 0.5 * product(inv, cur))
-        current[...] = product(cur, mid)
-        inverse[...] = product(mid, inv)
+        iterates[...] = product((high, low), mid)
         return carry
 
     lax.fori_loop(0, ITERS - 2, newton, 0)
@@ -532,9 +531,9 @@
         copy.wait()
     innovation = functools.reduce(jnp.add, [push_role[r] for r in range(n_role)])
     innovation = jnp.broadcast_to(innovation, (GROUP, total))
-    inv = halves(inverse[...])
-    mid = halves(jnp.where(diagonal, 1.5, 0.0) - 0.5 * product(inv, halves(current[...])))
-    root = product(mid, inv)
+    inv = halves(iterates[total:])
+    mid = halves(jnp.where(diagonal, 1.5, 0.0) - 0.5 * product(inv, halves(iterates[:total])))
+    root = product(inv, mid)
     root_halves = halves(root)
     shifted = product(halves(product(halves(innovation), root_halves)), root_halves) / scaling
     mixing[...] = root * jnp.sqrt((total - 1.0) / scaling) + shifted[0:1, :]
@@ -625,8 +624,7 @@
             vmem(n_role, 1, total),
             vmem(gram_rows, total),
             vmem(total, total),
-            vmem(total, total),
-            vmem(total, total),
+            vmem(2 * total, total),
             vmem(total, total),
             vmem(total, chunk * cols, dtype=BF16),
             vmem(total, chunk * cols, dtype=BF16),

time: 79.6 us -> 80.8 us (1.015)
  Pallas kernels: 77.2 us -> 78.4 us
    pallas_call x1, Pallas kernels: 77.2 us -> 78.4 us  [shards(): pl.pallas_call(functools.partial(kernel, (n_member, n_domain, n_role, mem...]
where the time goes in v5:
time: 80.8 us; the launch traced here: 80.7 us
  Pallas kernels  78.4 us (97%)
  local copies, waits for them, and re-layouts  1.58 us (2%)
    pallas_call x1, Pallas kernels, shards(): pl.pallas_call(functools.partial(kernel, (n_member, n_domain, n_role, mem...  78.4 us

profile of v5, /device:TPU:1, one launch (start us, length us, event | category | flops | bytes accessed | tf_op | source)
XLA Modules:
  0.0 80.7 jit_solution(5363041891563255241)
XLA Ops:
  0.7 78.4 %forecast_analysis.1 = f32[64,32,128]{2,1,0:T(8,128)S(1)} custom-call(s32[1]{0:T(128)S(6)} %copy.10.count_ref, f32[2048,128]{1,0:T(8,128)} %bitcast.6, f32[64,128]{1,0:T(8,128)} %diffusion_hbm.1, f32[64,128]{1,0:T(8,128)} %drift_rows_hbm.1, f32[64,128]{1,0:T(8,128)} %drift_cols_hbm.1, s32[8,128]{1,0:T(8,128)} %bitcast.7, f32[8,128]{1,0:T(8,128)} %bitcast.8, ...), custom_call_target="tpu_custom_call" | custom-call | tf_op jit(solution)/shard_map/forecast_analysis/pallas_call | solution.py:590
  79.1 1.6 %copy.9 = f32[32,64,128]{2,1,0:T(8,128)} copy(f32[32,64,128]{2,0,1:T(8,128)S(1)} %bitcast.5) | data formatting | bytes 2097152 | tf_op jit(solution)/shard_map/transpose | solution.py:660
